TPU v7x, 128 devices: a whole 4x4x4 slice. The times are simulated.
128 devices in a mesh: req: 16 (over y, x), seq: 4 (over z), hid: 2 (over core).
Axes of the slice: x: 4, y: 4, z: 4, core: 2. Of those that a mesh axis runs over, the one named last changes fastest.
Arguments:
- tokens: bfloat16 [65536, 2048], P(('req', 'seq')), may hold values from -6 to 6
- attention_gain: bfloat16 [2048], replicated, may hold values from 0.099609375 to 1.8984375
- project_weight: bfloat16 [2048, 2048], P(None, 'hid'), may hold values from -0.125 to 0.125
- conv_weight: bfloat16 [4, 2048], P(None, 'hid'), may hold values from -3 to 3
- decay_down: bfloat16 [2048, 16], replicated, may hold values from -0.125 to 0.125
- decay_up: bfloat16 [16, 512], P(None, 'hid'), may hold values from -1.5 to 1.5
- decay_bias: float32 [512], P('hid'), may hold values from -2 to 10
- output_gate: bfloat16 [2048, 1024], P(None, 'hid'), may hold values from -0.125 to 0.125
- head_gain: bfloat16 [512], replicated, may hold values from 0.099609375 to 1.8984375
- output_weight: bfloat16 [1024, 2048], P('hid'), may hold values from -0.1875 to 0.1875
- mixer_gain: bfloat16 [2048], replicated, may hold values from 0.099609375 to 1.8984375
- gate_weight: bfloat16 [2048, 2816], P('req', 'hid'), may hold values from -0.125 to 0.125
- up_weight: bfloat16 [2048, 2816], P('req', 'hid'), may hold values from -0.125 to 0.125
- down_weight: bfloat16 [2816, 2048], P('hid', 'req'), may hold values from -0.109375 to 0.109375
- prompt_pages: int32 [16, 16], P('req'), may hold values from 0 to 64, as said below
- prompt_start: int32 [16, 16], P('req'), may hold values from 0 to 63, as said below
Outputs:
- hidden_out: bfloat16 [65536, 2048], P(('req', 'seq', 'hid'))
- page_states: bfloat16 [1024, 2, 256, 512], P(('req', 'seq'), 'hid')
- conv_edges: bfloat16 [1024, 3, 2048], P(('req', 'seq'), None, 'hid')
Inputs may be any that keep to these rules, and one draw needn't show every extreme that they name: `prompt_pages`: row r lists the page counts of the prompts of group r; 0 marks an unused slot; in every draw some group holds one prompt of all its 64 pages. `prompt_start`: the slots of a row that are used cover pages in increasing order without intersection and end by page 64; pages between prompts belong to none; an unused slot starts at page 64 - 1, and every draw has one.
All inputs are finite; a program needn't handle non-finite values.
Results may differ from a plain program's by a relative error of at most 0.014.
Values may be sent and summed in bfloat16 or wider, within the bound.
A program may use at most 192 MiB of HBM per device.

v0:
```python
import functools

import jax
import jax.numpy as jnp
from jax import lax
from jax.experimental.layout import Layout, with_layout_constraint
from jax.sharding import PartitionSpec as P
from jax.experimental import pallas as pl
from jax.experimental.pallas import tpu as pltpu

HK = 256
HV = 512
KCONV = 4
PAGE = 64
CONVW = 1024


EPSILON = 1e-06
TOP_PRECISION = lax.Precision.HIGHEST


def shifted(value, axis, steps):
    count = lax.axis_size(axis)
    first, last = (max(0, -steps), min(count, count - steps))
    return lax.ppermute(value, axis, [(source, source + steps) for source in range(first, last)])


def prefix_2(array, axis, join, neutral):
    place = lax.axis_index(axis)
    decay, memory = array
    width = memory.shape[-1]
    packed = jnp.concatenate(
        [memory.reshape(-1, width), jnp.pad(decay.reshape(1, -1), ((0, 0), (0, width - decay.size)))],
        axis=0,
    ).astype(jnp.bfloat16)
    received = spread_over_seq(packed)
    gathered = (
        received[:, -1, : decay.size].reshape((-1,) + decay.shape),
        received[:, :-1].reshape((-1,) + memory.shape),
    )
    state = jax.tree.map(lambda a, e: jnp.zeros_like(a) + jnp.asarray(e, a.dtype), array, neutral)

    def one(lap, state):
        return join(
            state,
            jax.tree.map(
                lambda a, own: lax.dynamic_index_in_dim(a, lap, 0, False).astype(own.dtype),
                gathered,
                array,
            ),
        )

    return lax.fori_loop(0, place, one, state)


def partner_kernel(rows, src_ref, dst_ref, send_sem, recv_sem):
    partner = 1 - lax.axis_index("hid")
    barrier = pltpu.get_barrier_semaphore()
    pl.semaphore_signal(
        barrier, inc=1, device_id={"hid": partner}, device_id_type=pl.DeviceIdType.MESH
    )
    pl.semaphore_wait(barrier, 1)
    start = pl.multiple_of(partner * rows, rows) if rows < src_ref.shape[0] else 0
    copy = pltpu.make_async_remote_copy(
        src_ref=src_ref.at[pl.ds(start, rows)],
        dst_ref=dst_ref,
        send_sem=send_sem,
        recv_sem=recv_sem,
        device_id={"hid": partner},
        device_id_type=pl.DeviceIdType.MESH,
    )
    copy.start()
    copy.wait()


def from_partner(value, rows, kernel_id):
    return pl.pallas_call(
        functools.partial(partner_kernel, rows),
        out_shape=jax.ShapeDtypeStruct((rows,) + value.shape[1:], value.dtype),
        in_specs=[pl.BlockSpec(memory_space=pl.ANY)],
        out_specs=pl.BlockSpec(memory_space=pl.ANY),
        scratch_shapes=[pltpu.SemaphoreType.DMA, pltpu.SemaphoreType.DMA],
        compiler_params=pltpu.CompilerParams(collective_id=kernel_id, has_side_effects=True),
    )(value)


def spread_kernel(src_ref, dst_ref, send_sem, recv_sem):
    count = lax.axis_size("seq")
    me = lax.axis_index("seq")
    barrier = pltpu.get_barrier_semaphore()
    for step in range(1, count):
        pl.semaphore_signal(
            barrier,
            inc=1,
            device_id={"seq": lax.rem(me + step, count)},
            device_id_type=pl.DeviceIdType.MESH,
        )
    pl.semaphore_wait(barrier, count - 1)
    copies = []
    for step in range(1, count):
        copy = pltpu.make_async_remote_copy(
            src_ref=src_ref,
            dst_ref=dst_ref.at[me],
            send_sem=send_sem.at[step - 1],
            recv_sem=recv_sem.at[me],
            device_id={"seq": jnp.minimum(me + step, count - 1)},
            device_id_type=pl.DeviceIdType.MESH,
        )
        copies.append(copy)

        @pl.when(me + step < count)
        def _():
            copy.start()

    for step, copy in zip(range(1, count), copies):

        @pl.when(me + step < count)
        def _():
            copy.wait_send()

    for step in range(1, count):
        source = jnp.maximum(me - step, 0)

        @pl.when(me - step >= 0)
        def _():
            pltpu.make_async_remote_copy(
                src_ref=src_ref,
                dst_ref=dst_ref.at[source],
                send_sem=send_sem.at[step - 1],
                recv_sem=recv_sem.at[source],
                device_id={"seq": source},
                device_id_type=pl.DeviceIdType.MESH,
            ).wait_recv()


def spread_over_seq(value):
    count = lax.axis_size("seq")
    return pl.pallas_call(
        spread_kernel,
        out_shape=jax.ShapeDtypeStruct((count,) + value.shape, value.dtype),
        in_specs=[pl.BlockSpec(memory_space=pl.ANY)],
        out_specs=pl.BlockSpec(memory_space=pl.ANY),
        scratch_shapes=[
            pltpu.SemaphoreType.DMA((count - 1,)),
            pltpu.SemaphoreType.DMA((count,)),
        ],
        compiler_params=pltpu.CompilerParams(collective_id=2, has_side_effects=True),
    )(value)


def recurrence_kernel(decay_ref, carried_ref, terms_ref, out_ref, previous_ref, state_ref):
    step = pl.program_id(0)
    chunk = terms_ref.shape[0]
    reach = terms_ref.shape[-1] // decay_ref.shape[-1]

    @pl.when(step == 0)
    def _():
        state_ref[...] = jnp.zeros_like(state_ref)

    for page in range(chunk):
        kept = jnp.concatenate([carried_ref[page]] * reach, axis=-1) * state_ref[...]
        previous_ref[page] = kept
        state = jnp.concatenate([decay_ref[page]] * reach, axis=-1) * kept + terms_ref[page]
        state_ref[...] = state
        out_ref[page] = state


def page_recurrence(decay, carried, terms, chunk=4):
    page_count, rows, width = terms.shape
    lanes = decay.shape[-1]
    block = pl.BlockSpec((chunk, rows, width), lambda p: (p, 0, 0))
    flags = pl.BlockSpec((chunk, rows, lanes), lambda p: (p, 0, 0))
    return pl.pallas_call(
        recurrence_kernel,
        out_shape=(
            jax.ShapeDtypeStruct(terms.shape, terms.dtype),
            jax.ShapeDtypeStruct(terms.shape, terms.dtype),
        ),
        grid=(page_count // chunk,),
        in_specs=[flags, flags, block],
        out_specs=(block, block),
        scratch_shapes=[pltpu.VMEM((rows, width), jnp.float32)],
    )(decay, carried, terms)


def rms_scaled(values, scale_gain):
    values = values.astype(jnp.float32)
    return (
        values
        * lax.rsqrt(jnp.mean(values * values, axis=-1, keepdims=True) + EPSILON)
        * scale_gain.astype(jnp.float32)
    )


def page_segments(page_counts, starts, total_pages):
    position = jnp.arange(total_pages, dtype=jnp.int32)
    inside = (position[None, :] >= starts[:, None]) & (
        position[None, :] < starts[:, None] + page_counts[:, None]
    )
    labels = jnp.arange(1, page_counts.shape[0] + 1, dtype=jnp.int32)
    segment = jnp.sum(jnp.where(inside, labels[:, None], 0), axis=0) - 1
    earlier = jnp.concatenate([jnp.full((1,), -1, jnp.int32), segment[:-1]])
    return ((segment == earlier) & (segment >= 0)).astype(jnp.float32)


def short_conv(by_page, before, carried, conv_taps):
    kept_rows = before.astype(jnp.float32) * carried[:, None, None]
    widened = jnp.concatenate([kept_rows, by_page.astype(jnp.float32)], axis=1)
    tap_count = conv_taps.shape[0]
    length = by_page.shape[1]
    result = jnp.zeros(by_page.shape, jnp.float32)
    for offset in range(tap_count):
        result = (
            result
            + conv_taps[offset].astype(jnp.float32)
            * widened[:, tap_count - 1 - offset : tap_count - 1 - offset + length]
        )
    return result


def split_features(mixed_rows, key_width):
    query_rows = jax.nn.silu(mixed_rows[..., :key_width])
    key_rows = jax.nn.silu(mixed_rows[..., key_width : 2 * key_width]) * key_width ** (-0.5)
    value_matrix = mixed_rows[..., 2 * key_width :]
    return (
        query_rows.transpose(0, 2, 1, 3),
        key_rows.transpose(0, 2, 1, 3),
        value_matrix.transpose(0, 2, 1, 3),
    )


def page_block(query_rows, key_rows, value_matrix, decay_sum, carried):
    length = query_rows.shape[2]
    page_count = query_rows.shape[0]
    raised_rows = query_rows * jnp.exp(decay_sum)
    lowered = key_rows * jnp.exp(-decay_sum)
    scores = jnp.einsum("phik,phjk->phij", raised_rows, lowered, precision=TOP_PRECISION)
    rows_index = jnp.arange(length)
    causal = rows_index[:, None] >= rows_index[None, :]
    scores = jnp.where(causal[None, None], scores, 0.0)
    layer_output = jnp.einsum("phij,phjv->phiv", scores, value_matrix, precision=TOP_PRECISION)
    closing_sum = decay_sum[:, :, -1, :]
    weighted_rows = key_rows * jnp.exp(closing_sum[:, :, None, :] - decay_sum)
    page_terms = jnp.einsum(
        "phte,phtb->pheb", weighted_rows, value_matrix, precision=TOP_PRECISION
    )
    lanes = 128
    rows = closing_sum.shape[1] * closing_sum.shape[2]
    memories, previous = page_recurrence(
        jnp.broadcast_to(jnp.exp(closing_sum).reshape(page_count, rows, 1), (page_count, rows, lanes)),
        jnp.broadcast_to(carried[:, None, None], (page_count, rows, lanes)),
        page_terms.reshape(page_count, rows, page_terms.shape[-1]),
    )
    memories = memories.reshape(page_terms.shape)
    previous = previous.reshape(page_terms.shape)
    layer_output = layer_output + jnp.einsum(
        "phik,phkv->phiv", raised_rows, previous, precision=TOP_PRECISION
    )
    return memories[-1], layer_output, memories


def on_device(
    tokens,
    attention_gain,
    project_weight,
    conv_weight,
    decay_down,
    decay_up,
    decay_bias,
    output_gate,
    head_gain,
    output_weight,
    mixer_gain,
    gate_weight,
    up_weight,
    down_weight,
    prompt_pages,
    prompt_start,
):
    token_count = tokens.shape[0]
    page_count = token_count // PAGE
    local_heads = project_weight.shape[1] // CONVW
    rim_rows = KCONV - 1
    seq_index = lax.axis_index("seq")
    group_pages = page_count * lax.axis_size("seq")
    page_flags = page_segments(prompt_pages[0], prompt_start[0], group_pages)
    carried = lax.dynamic_slice_in_dim(page_flags, seq_index * page_count, page_count)
    normed = rms_scaled(tokens, attention_gain).astype(jnp.bfloat16)
    projected = jnp.dot(normed, project_weight, preferred_element_type=jnp.float32).astype(
        jnp.bfloat16
    )
    by_page = projected.reshape(page_count, PAGE, local_heads * CONVW)
    incoming = shifted(by_page[-1, PAGE - rim_rows :], "seq", 1)
    before = jnp.concatenate([incoming[None], by_page[:-1, PAGE - rim_rows :]], axis=0)
    mixed_rows = short_conv(by_page, before, carried, conv_weight).reshape(
        page_count, PAGE, local_heads, CONVW
    )
    query_rows, key_rows, value_matrix = split_features(mixed_rows, HK)
    lowrank = jnp.dot(normed, decay_down, preferred_element_type=jnp.float32).astype(jnp.bfloat16)
    decay_log = (
        jax.nn.log_sigmoid(
            jnp.dot(lowrank, decay_up, preferred_element_type=jnp.float32) + decay_bias
        )
        / 16.0
    )
    decay_log = decay_log.reshape(page_count, PAGE, local_heads, HK).transpose(0, 2, 1, 3)
    decay_sum = jnp.cumsum(decay_log, axis=2)
    local_memory, outputs, memories = page_block(
        query_rows, key_rows, value_matrix, decay_sum, carried
    )
    totals = decay_sum[:, :, -1, :]
    through = jnp.cumsum(totals, axis=0)
    alive_mask = jnp.cumprod(carried)
    block_decay = alive_mask[-1] * jnp.exp(through[-1])

    def compose(earlier, latter):
        return (earlier[0] * latter[0], latter[0][..., None] * earlier[1] + latter[1])

    prefix = prefix_2(
        (block_decay, local_memory),
        "seq",
        compose,
        (jnp.ones_like(block_decay), jnp.zeros_like(local_memory)),
    )
    incoming_state = prefix[1]
    before_sum = through - totals
    extent_factor = alive_mask[:, None, None, None] * jnp.exp(decay_sum + before_sum[:, :, None, :])
    outputs = outputs + jnp.einsum(
        "dlof,lfg->dlog", query_rows * extent_factor, incoming_state, precision=TOP_PRECISION
    )
    memories = (
        memories + (alive_mask[:, None, None] * jnp.exp(through))[..., None] * incoming_state[None]
    )
    attended = outputs.transpose(0, 2, 1, 3).reshape(token_count, local_heads, HV)
    normed_heads = rms_scaled(attended, head_gain)
    opening = jax.nn.silu(jnp.dot(normed, output_gate, preferred_element_type=jnp.float32)).reshape(
        token_count, local_heads, HV
    )
    gated_rows = (
        (normed_heads * opening).astype(jnp.bfloat16).reshape(token_count, local_heads * HV)
    )
    partial_value = jnp.dot(gated_rows, output_weight, preferred_element_type=jnp.float32)
    half_rows = token_count // lax.axis_size("hid")
    row_start = lax.axis_index("hid") * half_rows
    own_value = partial_value.astype(jnp.bfloat16)
    mixed_sum = own_value.astype(jnp.float32) + from_partner(own_value, token_count, 0).astype(
        jnp.float32
    )
    residual = (tokens.astype(jnp.float32) + mixed_sum).astype(jnp.bfloat16)
    feed_in = rms_scaled(residual, mixer_gain).astype(jnp.bfloat16)
    own_residual = lax.dynamic_slice_in_dim(residual, row_start, half_rows, 0)

    def widen(weight_rows):
        return jnp.dot(feed_in, weight_rows, preferred_element_type=jnp.float32)

    width = gate_weight.shape[1]
    both_part = widen(
        lax.all_gather(
            jnp.concatenate([gate_weight, up_weight], axis=1), "req", axis=0, tiled=True
        )
    )
    gate_part = both_part[:, :width]
    up_part = both_part[:, width:]
    hidden = lax.optimization_barrier((jax.nn.silu(gate_part) * up_part).astype(jnp.bfloat16))
    down_block = with_layout_constraint(down_weight.T, Layout((0, 1)))
    down_rows = lax.all_gather(down_block, "req", axis=0, tiled=True)
    partials = lax.dot_general(
        hidden, down_rows, (((1,), (1,)), ((), ())), preferred_element_type=jnp.float32
    )
    own_partials = partials.astype(jnp.bfloat16)
    feed_sum = lax.dynamic_slice_in_dim(own_partials, row_start, half_rows, 0).astype(
        jnp.float32
    ) + from_partner(own_partials, half_rows, 1).astype(jnp.float32)
    result = (own_residual.astype(jnp.float32) + feed_sum).astype(jnp.bfloat16)
    return (result, memories.astype(jnp.bfloat16), by_page[:, PAGE - rim_rows :])


def solution(mesh):
    return jax.shard_map(
        on_device,
        mesh=mesh,
        in_specs=(
            P(("req", "seq"), None),
            P(),
            P(None, "hid"),
            P(None, "hid"),
            P(),
            P(None, "hid"),
            P("hid"),
            P(None, "hid"),
            P(),
            P("hid", None),
            P(),
            P("req", "hid"),
            P("req", "hid"),
            P("hid", "req"),
            P("req", None),
            P("req", None),
        ),
        out_specs=(
            P(("req", "seq", "hid"), None),
            P(("req", "seq"), "hid", None, None),
            P(("req", "seq"), None, "hid"),
        ),
        check_vma=False,
    )
```

profile of v0, /device:TPU:99, one launch (start us, length us, event | category | flops | bytes accessed | tf_op | source)
XLA Modules:
  0.0 203.5 jit_solution(3116698297995768011)
XLA Ops:
  10.3 3.3 %fusion.3 = f32[1024]{0:T(1024)S(1)} fusion(bf16[1024,2048]{1,0:T(8,128)(2,1)} %param.18), kind=kLoop, calls=%fused_computation.10 | loop fusion | flops 6290432 | bytes 4198400 | tf_op jit(solution)/shard_map/reduce_sum | solution.py:190
  13.6 7.3 %convolution_convert_fusion.2 = bf16[1024,1024]{1,0:T(8,128)(2,1)S(1)} fusion(bf16[2048,1024]{1,0:T(8,128)(2,1)} %param.20, bf16[1024,2048]{1,0:T(8,128)(2,1)S(1)} %copy-done.5, f32[2048]{0:T(1024)S(1)} %convert_element_type.151, f32[1024]{0:T(1024)S(1)} %add_rsqrt_fusion.2), kind=kOutput, calls=%fused_computation.48 | convolution fusion | flops 4304404480 | bytes 10498048 | tf_op jit(solution)/shard_map/dot_general | solution.py:289
  24.9 5.2 %fusion.29 = f32[1024,256]{1,0:T(8,128)} fusion(bf16[16,256]{1,0:T(8,128)(2,1)S(1)} %copy-done.14, bf16[2048,16]{0,1:T(8,128)(2,1)S(1)} %copy-done.13, f32[256]{0:T(256)S(1)} %copy-done.15, bf16[1024,2048]{1,0:T(8,128)(2,1)} %param.18, f32[2048]{0:T(1024)S(1)} %convert_element_type.151, f32[1024]{0:T(1024)S(1)} %add_rsqrt_fusion.2), kind=kOutput, calls=%fused_computation.54 | convolution fusion | flops 86523904 | bytes 5329920 | tf_op jit(solution)/shard_map/dot_general | solution.py:302
  35.0 4.1 %convert_element_type.154 = f32[16,64,1024]{2,1,0:T(8,128)} convert(bf16[16,64,1024]{2,1,0:T(8,128)(2,1)} %bitcast.137) | non-fusion elementwise | flops 1048576 | bytes 6291456 | tf_op jit(solution)/shard_map/convert_element_type | solution.py:208
  40.9 7.4 %fusion.12 = f32[16,64,1,1024]{3,1,0,2:T(8,128)S(1)} fusion(f32[16,64,1024]{2,1,0:T(8,128)} %convert_element_type.154, f32[16,3,1024]{2,1,0:T(4,128)S(1)} %convert_multiply_fusion.4, f32[1024]{0:T(1024)S(1)} %bitcast.144, f32[1024]{0:T(1024)S(1)} %bitcast.145, f32[1024]{0:T(1024)S(1)} %bitcast.143, f32[1024]{0:T(1024)S(1)} %bitcast.142), kind=kLoop, calls=%fused_computation.25 | loop fusion | flops 10485760 | bytes 8601600 | tf_op jit(solution)/shard_map/reshape | solution.py:295
  48.3 9.3 %fusion.25.terms_ref = f32[16,256,512]{2,1,0:T(8,128)} fusion(f32[16,64,1,1024]{3,1,0,2:T(8,128)S(1)} %fusion.12, f32[16,1,64,256]{3,0,1,2:T(8,128)S(1)} %fusion.40, f32[16,256]{1,0:T(8,128)S(1)} %get-tuple-element.89), kind=kOutput, calls=%fused_computation.46 | convolution fusion | flops 1612447744 | bytes 12599296 | tf_op jit(solution)/shard_map/phte,phtb->pheb/dot_general | solution.py:244
  61.1 11.3 %shard_map.175 = (f32[16,256,512]{2,1,0:T(8,128)}, f32[16,256,512]{2,1,0:T(8,128)}) custom-call(f32[16,256,128]{2,1,0:T(8,128)} %broadcast_in_dim.38.decay_ref, f32[16,256,128]{2,1,0:T(8,128)} %broadcast_in_dim.39.carried_ref, f32[16,256,512]{2,1,0:T(8,128)} %fusion.25.terms_ref), custom_call_target="tpu_custom_call" | custom-call | tf_op jit(solution)/shard_map/pallas_call | solution.py:173
  74.2 17.8 %shard_map.176 = bf16[4,257,512]{2,1,0:T(8,128)(2,1)} custom-call(bf16[257,512]{1,0:T(8,128)(2,1)} %fusion.54.src_ref), custom_call_target="tpu_custom_call" | custom-call | tf_op jit(solution)/shard_map/pallas_call | solution.py:138
  92.1 2.3 %slice_bitcast_fusion.3 = bf16[4,1,256,512]{3,2,1,0:T(8,128)(2,1)} fusion(bf16[4,257,512]{2,1,0:T(8,128)(2,1)} %shard_map.176), kind=kLoop, calls=%fused_computation.70 | loop fusion | bytes 2097152 | tf_op jit(solution)/shard_map/while | solution.py:53
  95.1 4.2 %convolution_select_fusion = f32[16,64,64]{2,1,0:T(8,128)S(1)} fusion(f32[16,1,64,256]{3,0,1,2:T(8,128)S(1)} %fusion.40, pred[64,64]{1,0:T(8,128)(4,1)S(1)} %iota_compare_fusion.1, f32[16,64,1,1024]{3,1,0,2:T(8,128)} %copy-done.2), kind=kOutput, calls=%fused_computation.51 | convolution fusion | flops 204537856 | bytes 4464640 | tf_op jit(solution)/shard_map/phik,phjk->phij/dot_general | solution.py:237
  99.3 3.1 %fusion.26 = f32[16,64,512]{2,1,0:T(8,128)} fusion(f32[16,64,64]{2,1,0:T(8,128)S(1)} %convolution_select_fusion, f32[16,64,1,1024]{3,1,0,2:T(8,128)S(1)} %copy-done.3), kind=kOutput, calls=%fused_computation.47 | convolution fusion | flops 402653184 | bytes 4718592 | tf_op jit(solution)/shard_map/phij,phjv->phiv/dot_general | solution.py:241
  102.4 10.6 %fusion.42 = f32[16,64,512]{2,1,0:T(8,128)} fusion(f32[16,256,512]{2,1,0:T(8,128)} %get-tuple-element.49, f32[16,1,64,256]{3,0,1,2:T(8,128)S(1)} %fusion.40, f32[16,64,1,1024]{3,1,0,2:T(8,128)S(1)} %copy-done.3), kind=kOutput, calls=%fused_computation.73 | convolution fusion | flops 1611923456 | bytes 12582912 | tf_op jit(solution)/shard_map/phik,phkv->phiv/dot_general | solution.py:256
  113.1 3.6 %while.12 = (s32[]{:T(128)}, f32[1,256,512]{2,1,0:T(8,128)S(1)}, s32[]{:T(128)}, bf16[4,1,256]{2,1,0:T(2,128)(2,1)S(1)}, bf16[4,1,256,512]{3,2,1,0:T(8,128)(2,1)}, /*index=5*/s32[]{:T(128)}, s32[]{:T(128)}, s32[]{:T(128)}) while((s32[]{:T(128)}, f32[1,256,512]{2,1,0:T(8,128)S(1)}, s32[]{:T(128)}, bf16[4,1,256]{2,1,0:T(2,128)(2,1)S(1)}, ...), condition=%wide.region_6.7_spmd, body=%wide.region_5.6_spmd.sunk | while | flops 393477 | bytes 1313407 | solution.py:53
  116.7 6.9 %multiply_reduce_fusion = (f32[16,64]{1,0:T(8,128)S(1)}, f32[16,1,64,512]{3,2,0,1:T(8,128)}) fusion(f32[16,1,64,256]{3,0,1,2:T(8,128)} %copy-done.4, f32[16,256]{1,0:T(8,128)S(1)} %get-tuple-element.88, f32[16]{0:T(128)S(1)} %reduce.2, f32[16,64,1,1024]{3,1,0,2:T(8,128)} %copy-done.2, f32[1,256,512]{2,1,0:T(8,128)S(1)} %get-tuple-element.51, ...), kind=kOutput, calls=%fused_computation.45 | convolution fusion | flops 1614543872 | bytes 8933440 | tf_op jit(solution)/shard_map/dlof,lfg->dlog/dot_general | solution.py:328
  123.7 6.2 %fusion.24 = bf16[1024,512]{1,0:T(8,128)(2,1)S(1)} fusion(f32[16,1,64,512]{3,2,0,1:T(8,128)} %get-tuple-element.95, f32[512]{0:T(512)S(1)} %convert_element_type.164, f32[1024]{0:T(1024)S(1)} %rsqrt.29, bf16[2048,512]{1,0:T(8,128)(2,1)} %param.25, bf16[1024,2048]{1,0:T(8,128)(2,1)} %param.18, f32[2048]{0:T(1024)S(1)} %convert_element_type.151, ...), kind=kOutput, calls=%fused_computation.44 | convolution fusion | flops 2160066560 | bytes 9455616 | tf_op jit(solution)/shard_map/dot_general | solution.py:336
  129.8 4.4 %convolution_convert_fusion.1.src_ref = bf16[1024,2048]{1,0:T(8,128)(2,1)} fusion(bf16[1024,512]{1,0:T(8,128)(2,1)S(1)} %fusion.24, bf16[512,2048]{1,0:T(8,128)(2,1)S(1)} %copy-done), kind=kOutput, calls=%fused_computation.37 | convolution fusion | flops 2149580800 | bytes 7340032 | tf_op jit(solution)/shard_map/dot_general | solution.py:342
  134.2 7.7 %shard_map.177 = bf16[1024,2048]{1,0:T(8,128)(2,1)} custom-call(bf16[1024,2048]{1,0:T(8,128)(2,1)} %convolution_convert_fusion.1.src_ref), custom_call_target="tpu_custom_call" | custom-call | tf_op jit(solution)/shard_map/pallas_call | solution.py:77
  141.9 7.7 %fusion = (f32[1024]{0:T(1024)S(1)}, bf16[1024,2048]{1,0:T(8,128)(2,1)}) fusion(bf16[1024,2048]{1,0:T(8,128)(2,1)} %shard_map.177, bf16[1024,2048]{1,0:T(8,128)(2,1)} %convolution_convert_fusion.1.src_ref, bf16[1024,2048]{1,0:T(8,128)(2,1)} %param.18), kind=kLoop, calls=%fused_computation.7 | loop fusion | flops 18873344 | bytes 16781312 | tf_op jit(solution)/shard_map/reduce_sum | solution.py:190
  149.6 5.3 %fusion.16 = bf16[16,1,256,512]{3,2,1,0:T(8,128)(2,1)} fusion(f32[16,256,512]{2,1,0:T(8,128)} %get-tuple-element.50, f32[256,512]{1,0:T(8,128)S(1)} %bitcast.134, f32[16,256]{1,0:T(8,128)S(1)} %bitcast_multiply_fusion.5), kind=kLoop, calls=%fused_computation.29 | loop fusion | flops 6291456 | bytes 13123584
  154.9 17.5 %fusion.17 = f32[1024,2816]{1,0:T(8,128)S(1)} fusion(bf16[2048,2816]{1,0:T(8,128)(2,1)} %all-gather.3.cloned.1.call-done, bf16[1024,2048]{1,0:T(8,128)(2,1)} %get-tuple-element.87, f32[2048]{0:T(1024)S(1)} %convert_element_type.172, f32[1024]{0:T(1024)S(1)} %add_rsqrt_fusion.1), kind=kOutput, calls=%fused_computation.30 | convolution fusion | flops 11819548672 | bytes 27275264 | tf_op jit(solution)/shard_map/dot_general | solution.py:354
  172.4 2.9 %fusion.7 = bf16[1024,1408]{1,0:T(8,128)(2,1)} fusion(f32[1024,2816]{1,0:T(8,128)S(1)} %fusion.17), kind=kLoop, calls=%fused_computation.18 | loop fusion | flops 8650752 | bytes 14417920 | tf_op jit(solution)/shard_map/convert_element_type | solution.py:364
  175.4 10.9 %convolution_convert_fusion.src_ref = bf16[1024,2048]{1,0:T(8,128)(2,1)} fusion(bf16[1024,1408]{1,0:T(8,128)(2,1)} %fusion.7, bf16[2048,1408]{1,0:T(8,128)(2,1)} %all-gather.5.cloned.1.call-done), kind=kOutput, calls=%fused_computation.36 | convolution fusion | flops 5907677184 | bytes 12845056 | tf_op jit(solution)/shard_map/dot_general | solution.py:367
  186.3 4.6 %shard_map.178 = bf16[512,2048]{1,0:T(8,128)(2,1)} custom-call(bf16[1024,2048]{1,0:T(8,128)(2,1)} %convolution_convert_fusion.src_ref), custom_call_target="tpu_custom_call" | custom-call | tf_op jit(solution)/shard_map/pallas_call | solution.py:77
  190.9 5.6 %add_convert_fusion.1 = bf16[512,2048]{1,0:T(8,128)(2,1)} fusion(bf16[512,2048]{1,0:T(8,128)(2,1)} %shard_map.178, bf16[1024,2048]{1,0:T(8,128)(2,1)} %convolution_convert_fusion.src_ref, s32[]{:T(128)S(6)} %select_n.32, bf16[1024,2048]{1,0:T(8,128)(2,1)} %get-tuple-element.87), kind=kLoop, calls=%fused_computation.33 | loop fusion | flops 6291456 | bytes 8388612 | tf_op jit(solution)/shard_map/convert_element_type | solution.py:374
  (85 shorter events, 23.1 us)
Async XLA Ops:
  7.2 122.7 %copy-start = (bf16[512,2048]{1,0:T(8,128)(2,1)S(1)}, bf16[512,2048]{1,0:T(8,128)(2,1)}, u32[]{:S(2)}) copy-start(bf16[512,2048]{1,0:T(8,128)(2,1)} %param.27) | copy-start | bytes 6291460
  7.2 147.7 %all-gather.3.cloned.1.call-start = ((), (), s32[]{:S(2)}) async-start(), calls=%async_computation | async-start | bytes 12255232 | tf_op jit(solution)/shard_map/all_gather | solution.py:358
  9.4 166.0 %all-gather.5.cloned.1.call-start = ((), (), s32[]{:S(2)}) async-start(), calls=%async_computation.1 | async-start | bytes 6127616 | tf_op jit(solution)/shard_map/all_gather | solution.py:366
  9.4 4.1 %copy-start.5 = (bf16[1024,2048]{1,0:T(8,128)(2,1)S(1)}, bf16[1024,2048]{1,0:T(8,128)(2,1)}, u32[]{:S(2)}) copy-start(bf16[1024,2048]{1,0:T(8,128)(2,1)} %param.18) | copy-start | bytes 12582916
  13.6 10.2 %copy-start.7 = (bf16[1408,128]{1,0:T(8,128)(2,1)S(1)}, bf16[1408,128]{1,0:T(8,128)(2,1)}, u32[]{:S(2)}) copy-start(bf16[1408,128]{1,0:T(8,128)(2,1)} %param.31) | copy-start | bytes 1081348
  13.6 11.2 %copy-start.13 = (bf16[2048,16]{0,1:T(8,128)(2,1)S(1)}, bf16[2048,16]{0,1:T(8,128)(2,1)}, u32[]{:S(2)}) copy-start(bf16[2048,16]{0,1:T(8,128)(2,1)} %param.22) | copy-start | bytes 196612
  13.6 11.2 %copy-start.14 = (bf16[16,256]{1,0:T(8,128)(2,1)S(1)}, bf16[16,256]{1,0:T(8,128)(2,1)}, u32[]{:S(2)}) copy-start(bf16[16,256]{1,0:T(8,128)(2,1)} %param.23) | copy-start | bytes 24580
  13.6 11.2 %copy-start.15 = (f32[256]{0:T(256)S(1)}, f32[256]{0:T(256)}, u32[]{:S(2)}) copy-start(f32[256]{0:T(256)} %param.24) | copy-start | bytes 3076
  20.9 1.3 copy-start.6
  22.2 18.6 %collective-permute-start = (bf16[3,1024]{1,0:T(4,128)(2,1)S(1)}, bf16[3,1024]{1,0:T(4,128)(2,1)S(1)}, u32[]{:S(2)}, u32[]{:S(2)}) collective-permute-start(bf16[3,1024]{1,0:T(4,128)(2,1)S(1)} %slice_bitcast_fusion.6), channel_id=1, source_target_pairs={{0,2},{2,4},{4,6},{1,3},{3,5},{5,7},{8,10},{10,12},{12,14},{9,11},... | collective-permute-start | bytes 18440 | tf_op jit(solution)/shard_map/ppermute | solution.py:25
  24.8 7.2 %copy-start.10 = (s32[1,16]{1,0:T(1,128)S(1)}, s32[1,16]{1,0:T(1,128)}, u32[]{:S(2)}) copy-start(s32[1,16]{1,0:T(1,128)} %param.33) | copy-start | bytes 196
  24.8 7.2 %copy-start.12 = (s32[1,16]{1,0:T(1,128)S(1)}, s32[1,16]{1,0:T(1,128)}, u32[]{:S(2)}) copy-start(s32[1,16]{1,0:T(1,128)} %param.32) | copy-start | bytes 196
  24.8 7.3 %copy-start.8 = (bf16[4,1024]{1,0:T(4,128)(2,1)S(1)}, bf16[4,1024]{1,0:T(4,128)(2,1)}, u32[]{:S(2)}) copy-start(bf16[4,1024]{1,0:T(4,128)(2,1)} %param.21) | copy-start | bytes 24580
  30.1 10.0 %copy-start.11 = (bf16[512]{0:T(512)(128)(2,1)S(1)}, bf16[512]{0:T(512)(128)(2,1)}, u32[]{:S(2)}) copy-start(bf16[512]{0:T(512)(128)(2,1)} %param.26) | copy-start | bytes 3076
  30.1 10.0 %copy-start.9 = (bf16[2048]{0:T(1024)(128)(2,1)S(1)}, bf16[2048]{0:T(1024)(128)(2,1)}, u32[]{:S(2)}) copy-start(bf16[2048]{0:T(1024)(128)(2,1)} %param.28) | copy-start | bytes 12292
  32.0 70.5 %copy-start.4 = (f32[16,1,64,256]{3,0,1,2:T(8,128)}, f32[16,1,64,256]{3,0,1,2:T(8,128)S(1)}, u32[]{:S(2)}) copy-start(f32[16,1,64,256]{3,0,1,2:T(8,128)S(1)} %fusion.40) | copy-start | bytes 3145732
  48.3 9.3 %copy-start.2 = (f32[16,64,1,1024]{3,1,0,2:T(8,128)}, f32[16,64,1,1024]{3,1,0,2:T(8,128)S(1)}, u32[]{:S(2)}) copy-start(f32[16,64,1,1024]{3,1,0,2:T(8,128)S(1)} %fusion.12) | copy-start | bytes 12582916
  95.1 4.2 %copy-start.3 = (f32[16,64,1,1024]{3,1,0,2:T(8,128)S(1)}, f32[16,64,1,1024]{3,1,0,2:T(8,128)}, u32[]{:S(2)}) copy-start(f32[16,64,1,1024]{3,1,0,2:T(8,128)} %copy-done.2) | copy-start | bytes 12582916
  186.3 10.2 %copy-start.1 = (bf16[512,2048]{1,0:T(8,128)(2,1)S(1)}, bf16[512,2048]{1,0:T(8,128)(2,1)}, u32[]{:S(2)}) copy-start(bf16[512,2048]{1,0:T(8,128)(2,1)} %param.27) | copy-start | bytes 6291460
Sparse Core Ops, SparseCore 0:
  10.2 86.3 all-gather.2
  98.7 58.4 all-gather.4
where the time goes:
time: 207 us; the launch traced here: 204 us
  matrix products  85.5 us (41%)
  other arithmetic  46.5 us (22%)
  Pallas kernels  41.4 us (20%)
  between operations  14.7 us (7%)
  local copies, waits for them, and re-layouts  13.5 us (7%)
    pallas_call x1, Pallas kernels, spread_over_seq(): pl.pallas_call(spread_kernel, out_shape=jax.ShapeDtypeStruct((count,) + v...  17.8 us
    dot_general x1, matrix products, widen(): return jnp.dot(feed_in, weight_rows, preferred_element_type=jnp.float32)  17.5 us
    pallas_call x2, Pallas kernels, from_partner(): pl.pallas_call(functools.partial(partner_kernel, rows), out_shape=jax.Sha...  12.2 us
    pallas_call x1, Pallas kernels, page_recurrence(): pl.pallas_call(recurrence_kernel, out_shape=(jax.ShapeDtypeStruct(terms.s...  11.3 us
    reduce_sum x2, other arithmetic, rms_scaled(): jnp.mean(values * values, axis=-1, keepdims=True) + EPSILON  11 us
    dot_general x1, matrix products, on_device(): lax.dot_general(hidden, down_rows, (((1,), (1,)), ((), ())), preferred_el...  10.9 us
    dot_general x1, matrix products, page_block(): jnp.einsum('phik,phkv->phiv', raised_rows, previous, precision=TOP_PRECIS...  10.6 us
    dot_general x1, matrix products, page_block(): jnp.einsum('phte,phtb->pheb', weighted_rows, value_matrix, precision=TOP_...  9.27 us
  transfers between devices with their start and end apart: 3, of which 0 were waited for; matrix products, arithmetic and copies ran while one was open for 62% of the time, Pallas kernels for 18%

commit v1 on v0

--- a/solution.py
+++ b/solution.py
@@ -16,7 +16,7 @@
 
 
 EPSILON = 1e-06
-TOP_PRECISION = lax.Precision.HIGHEST
+TOP_PRECISION = lax.Precision.HIGH
 
 
 def shifted(value, axis, steps):

time: 207 us -> 195 us (0.942)
  the two profiles are of different devices: /device:TPU:99 before, /device:TPU:1 now
where the time goes in v1:
time: 195 us; the launch traced here: 193 us
  matrix products  77.8 us (40%)
  other arithmetic  43.9 us (23%)
  Pallas kernels  39.1 us (20%)
  between operations  14.4 us (7%)
  local copies, waits for them, and re-layouts  13.5 us (7%)
  starting transfers between devices  4.45 us (2%)
    dot_general x1, matrix products, widen(): return jnp.dot(feed_in, weight_rows, preferred_element_type=jnp.float32)  17.7 us
    pallas_call x1, Pallas kernels, spread_over_seq(): pl.pallas_call(spread_kernel, out_shape=jax.ShapeDtypeStruct((count,) + v...  15.3 us
    pallas_call x2, Pallas kernels, from_partner(): pl.pallas_call(functools.partial(partner_kernel, rows), out_shape=jax.Sha...  12.8 us
    reduce_sum x2, other arithmetic, rms_scaled(): jnp.mean(values * values, axis=-1, keepdims=True) + EPSILON  11 us
    dot_general x1, matrix products, on_device(): lax.dot_general(hidden, down_rows, (((1,), (1,)), ((), ())), preferred_el...  10.9 us
    pallas_call x1, Pallas kernels, page_recurrence(): pl.pallas_call(recurrence_kernel, out_shape=(jax.ShapeDtypeStruct(terms.s...  10.9 us
    dot_general x1, matrix products, page_block(): jnp.einsum('phik,phkv->phiv', raised_rows, previous, precision=TOP_PRECIS...  8.04 us
    reshape x1, other arithmetic, on_device(): short_conv(by_page, before, carried, conv_weight)  8.01 us
  transfers between devices with their start and end apart: 3, of which 0 were waited for; matrix products, arithmetic and copies ran while one was open for 60% of the time, Pallas kernels for 18%

profile of v1, /device:TPU:1, one launch (start us, length us, event | category | flops | bytes accessed | tf_op | source)
XLA Modules:
  0.0 193.5 jit_solution(15693579967062911528)
XLA Ops:
  10.3 3.3 %fusion.3 = f32[1024]{0:T(1024)S(1)} fusion(bf16[1024,2048]{1,0:T(8,128)(2,1)} %param.18), kind=kLoop, calls=%fused_computation.10 | loop fusion | flops 6290432 | bytes 4198400 | tf_op jit(solution)/shard_map/reduce_sum | solution.py:190
  13.6 7.3 %convolution_convert_fusion.2 = bf16[1024,1024]{1,0:T(8,128)(2,1)S(1)} fusion(bf16[2048,1024]{1,0:T(8,128)(2,1)} %param.20, bf16[1024,2048]{1,0:T(8,128)(2,1)S(1)} %copy-done.5, f32[2048]{0:T(1024)S(1)} %convert_element_type.151, f32[1024]{0:T(1024)S(1)} %add_rsqrt_fusion.2), kind=kOutput, calls=%fused_computation.48 | convolution fusion | flops 4304404480 | bytes 10498048 | tf_op jit(solution)/shard_map/dot_general | solution.py:289
  22.2 4.4 %collective-permute-start = (bf16[3,1024]{1,0:T(4,128)(2,1)S(1)}, bf16[3,1024]{1,0:T(4,128)(2,1)S(1)}, u32[]{:S(2)}, u32[]{:S(2)}) collective-permute-start(bf16[3,1024]{1,0:T(4,128)(2,1)S(1)} %slice_bitcast_fusion.6), channel_id=1, source_target_pairs={{0,2},{2,4},{4,6},{1,3},{3,5},{5,7},{8,10},{10,12},{12,14},{9,11},... | collective-permute-start | bytes 18440 | tf_op jit(solution)/shard_map/ppermute | solution.py:25
  27.6 5.2 %fusion.29 = f32[1024,256]{1,0:T(8,128)} fusion(bf16[16,256]{1,0:T(8,128)(2,1)S(1)} %copy-done.14, bf16[2048,16]{0,1:T(8,128)(2,1)S(1)} %copy-done.13, f32[256]{0:T(256)S(1)} %copy-done.15, bf16[1024,2048]{1,0:T(8,128)(2,1)} %param.18, f32[2048]{0:T(1024)S(1)} %convert_element_type.151, f32[1024]{0:T(1024)S(1)} %add_rsqrt_fusion.2), kind=kOutput, calls=%fused_computation.54 | convolution fusion | flops 86523904 | bytes 5329920 | tf_op jit(solution)/shard_map/dot_general | solution.py:302
  37.7 4.1 %convert_element_type.154 = f32[16,64,1024]{2,1,0:T(8,128)} convert(bf16[16,64,1024]{2,1,0:T(8,128)(2,1)} %bitcast.137) | non-fusion elementwise | flops 1048576 | bytes 6291456 | tf_op jit(solution)/shard_map/convert_element_type | solution.py:208
  43.7 8.0 %fusion.12 = f32[16,64,1,1024]{3,1,0,2:T(8,128)S(1)} fusion(f32[16,64,1024]{2,1,0:T(8,128)} %convert_element_type.154, f32[16,3,1024]{2,1,0:T(4,128)S(1)} %convert_multiply_fusion.4, f32[1024]{0:T(1024)S(1)} %bitcast.144, f32[1024]{0:T(1024)S(1)} %bitcast.145, f32[1024]{0:T(1024)S(1)} %bitcast.143, f32[1024]{0:T(1024)S(1)} %bitcast.142), kind=kLoop, calls=%fused_computation.25 | loop fusion | flops 10485760 | bytes 8601600 | tf_op jit(solution)/shard_map/reshape | solution.py:295
  51.7 6.1 %fusion.25.terms_ref = f32[16,256,512]{2,1,0:T(8,128)} fusion(f32[16,64,1,1024]{3,1,0,2:T(8,128)S(1)} %fusion.12, f32[16,1,64,256]{3,0,1,2:T(8,128)S(1)} %fusion.40, f32[16,256]{1,0:T(8,128)S(1)} %get-tuple-element.89), kind=kOutput, calls=%fused_computation.46 | convolution fusion | flops 807141376 | bytes 12599296 | tf_op jit(solution)/shard_map/phte,phtb->pheb/dot_general | solution.py:244
  61.3 10.9 %shard_map.175 = (f32[16,256,512]{2,1,0:T(8,128)}, f32[16,256,512]{2,1,0:T(8,128)}) custom-call(f32[16,256,128]{2,1,0:T(8,128)} %broadcast_in_dim.38.decay_ref, f32[16,256,128]{2,1,0:T(8,128)} %broadcast_in_dim.39.carried_ref, f32[16,256,512]{2,1,0:T(8,128)} %fusion.25.terms_ref), custom_call_target="tpu_custom_call" | custom-call | tf_op jit(solution)/shard_map/pallas_call | solution.py:173
  74.0 15.3 %shard_map.176 = bf16[4,257,512]{2,1,0:T(8,128)(2,1)} custom-call(bf16[257,512]{1,0:T(8,128)(2,1)} %fusion.54.src_ref), custom_call_target="tpu_custom_call" | custom-call | tf_op jit(solution)/shard_map/pallas_call | solution.py:138
  89.4 2.3 %slice_bitcast_fusion.3 = bf16[4,1,256,512]{3,2,1,0:T(8,128)(2,1)} fusion(bf16[4,257,512]{2,1,0:T(8,128)(2,1)} %shard_map.176), kind=kLoop, calls=%fused_computation.70 | loop fusion | bytes 2097152 | tf_op jit(solution)/shard_map/while | solution.py:53
  92.4 3.7 %convolution_select_fusion = f32[16,64,64]{2,1,0:T(8,128)S(1)} fusion(f32[16,1,64,256]{3,0,1,2:T(8,128)S(1)} %fusion.40, pred[64,64]{1,0:T(8,128)(4,1)S(1)} %iota_compare_fusion.1, f32[16,64,1,1024]{3,1,0,2:T(8,128)} %copy-done.2), kind=kOutput, calls=%fused_computation.51 | convolution fusion | flops 103874560 | bytes 4464640 | tf_op jit(solution)/shard_map/phik,phjk->phij/dot_general | solution.py:237
  96.1 2.4 %fusion.26 = f32[16,64,512]{2,1,0:T(8,128)} fusion(f32[16,64,64]{2,1,0:T(8,128)S(1)} %convolution_select_fusion, f32[16,64,1,1024]{3,1,0,2:T(8,128)S(1)} %copy-done.3), kind=kOutput, calls=%fused_computation.47 | convolution fusion | flops 201326592 | bytes 4718592 | tf_op jit(solution)/shard_map/phij,phjv->phiv/dot_general | solution.py:241
  98.5 8.0 %fusion.42 = f32[16,64,512]{2,1,0:T(8,128)} fusion(f32[16,256,512]{2,1,0:T(8,128)} %get-tuple-element.49, f32[16,1,64,256]{3,0,1,2:T(8,128)S(1)} %fusion.40, f32[16,64,1,1024]{3,1,0,2:T(8,128)S(1)} %copy-done.3), kind=kOutput, calls=%fused_computation.73 | convolution fusion | flops 806617088 | bytes 12582912 | tf_op jit(solution)/shard_map/phik,phkv->phiv/dot_general | solution.py:256
  106.8 5.9 %multiply_reduce_fusion = (f32[16,64]{1,0:T(8,128)S(1)}, f32[16,1,64,512]{3,2,0,1:T(8,128)}) fusion(f32[16,1,64,256]{3,0,1,2:T(8,128)} %copy-done.4, f32[16,256]{1,0:T(8,128)S(1)} %get-tuple-element.88, f32[16]{0:T(128)S(1)} %reduce.2, f32[16,64,1,1024]{3,1,0,2:T(8,128)} %copy-done.2, f32[1,256,512]{2,1,0:T(8,128)S(1)} %get-tuple-element.51, ...), kind=kOutput, calls=%fused_computation.45 | convolution fusion | flops 809237504 | bytes 8933440 | tf_op jit(solution)/shard_map/dlof,lfg->dlog/dot_general | solution.py:328
  112.9 6.2 %fusion.24 = bf16[1024,512]{1,0:T(8,128)(2,1)S(1)} fusion(f32[16,1,64,512]{3,2,0,1:T(8,128)} %get-tuple-element.95, f32[512]{0:T(512)S(1)} %convert_element_type.164, f32[1024]{0:T(1024)S(1)} %rsqrt.29, bf16[2048,512]{1,0:T(8,128)(2,1)} %param.25, bf16[1024,2048]{1,0:T(8,128)(2,1)} %param.18, f32[2048]{0:T(1024)S(1)} %convert_element_type.151, ...), kind=kOutput, calls=%fused_computation.44 | convolution fusion | flops 2160066560 | bytes 9455616 | tf_op jit(solution)/shard_map/dot_general | solution.py:336
  119.1 4.4 %convolution_convert_fusion.1.src_ref = bf16[1024,2048]{1,0:T(8,128)(2,1)} fusion(bf16[1024,512]{1,0:T(8,128)(2,1)S(1)} %fusion.24, bf16[512,2048]{1,0:T(8,128)(2,1)S(1)} %copy-done), kind=kOutput, calls=%fused_computation.37 | convolution fusion | flops 2149580800 | bytes 7340032 | tf_op jit(solution)/shard_map/dot_general | solution.py:342
  123.4 8.3 %shard_map.177 = bf16[1024,2048]{1,0:T(8,128)(2,1)} custom-call(bf16[1024,2048]{1,0:T(8,128)(2,1)} %convolution_convert_fusion.1.src_ref), custom_call_target="tpu_custom_call" | custom-call | tf_op jit(solution)/shard_map/pallas_call | solution.py:77
  131.7 7.7 %fusion = (f32[1024]{0:T(1024)S(1)}, bf16[1024,2048]{1,0:T(8,128)(2,1)}) fusion(bf16[1024,2048]{1,0:T(8,128)(2,1)} %shard_map.177, bf16[1024,2048]{1,0:T(8,128)(2,1)} %convolution_convert_fusion.1.src_ref, bf16[1024,2048]{1,0:T(8,128)(2,1)} %param.18), kind=kLoop, calls=%fused_computation.7 | loop fusion | flops 18873344 | bytes 16781312 | tf_op jit(solution)/shard_map/reduce_sum | solution.py:190
  139.5 5.4 %fusion.16 = bf16[16,1,256,512]{3,2,1,0:T(8,128)(2,1)} fusion(f32[16,256,512]{2,1,0:T(8,128)} %get-tuple-element.50, f32[256,512]{1,0:T(8,128)S(1)} %bitcast.134, f32[16,256]{1,0:T(8,128)S(1)} %bitcast_multiply_fusion.5), kind=kLoop, calls=%fused_computation.29 | loop fusion | flops 6291456 | bytes 13123584
  144.9 17.7 %fusion.17 = f32[1024,2816]{1,0:T(8,128)S(1)} fusion(bf16[2048,2816]{1,0:T(8,128)(2,1)} %all-gather.3.cloned.1.call-done, bf16[1024,2048]{1,0:T(8,128)(2,1)} %get-tuple-element.87, f32[2048]{0:T(1024)S(1)} %convert_element_type.172, f32[1024]{0:T(1024)S(1)} %add_rsqrt_fusion.1), kind=kOutput, calls=%fused_computation.30 | convolution fusion | flops 11819548672 | bytes 27275264 | tf_op jit(solution)/shard_map/dot_general | solution.py:354
  162.6 2.9 %fusion.7 = bf16[1024,1408]{1,0:T(8,128)(2,1)} fusion(f32[1024,2816]{1,0:T(8,128)S(1)} %fusion.17), kind=kLoop, calls=%fused_computation.18 | loop fusion | flops 8650752 | bytes 14417920 | tf_op jit(solution)/shard_map/convert_element_type | solution.py:364
  165.5 10.9 %convolution_convert_fusion.src_ref = bf16[1024,2048]{1,0:T(8,128)(2,1)} fusion(bf16[1024,1408]{1,0:T(8,128)(2,1)} %fusion.7, bf16[2048,1408]{1,0:T(8,128)(2,1)} %all-gather.5.cloned.1.call-done), kind=kOutput, calls=%fused_computation.36 | convolution fusion | flops 5907677184 | bytes 12845056 | tf_op jit(solution)/shard_map/dot_general | solution.py:367
  176.5 4.5 %shard_map.178 = bf16[512,2048]{1,0:T(8,128)(2,1)} custom-call(bf16[1024,2048]{1,0:T(8,128)(2,1)} %convolution_convert_fusion.src_ref), custom_call_target="tpu_custom_call" | custom-call | tf_op jit(solution)/shard_map/pallas_call | solution.py:77
  181.0 5.6 %add_convert_fusion.1 = bf16[512,2048]{1,0:T(8,128)(2,1)} fusion(bf16[512,2048]{1,0:T(8,128)(2,1)} %shard_map.178, bf16[1024,2048]{1,0:T(8,128)(2,1)} %convolution_convert_fusion.src_ref, s32[]{:T(128)S(6)} %select_n.32, bf16[1024,2048]{1,0:T(8,128)(2,1)} %get-tuple-element.87), kind=kLoop, calls=%fused_computation.33 | loop fusion | flops 6291456 | bytes 8388612 | tf_op jit(solution)/shard_map/convert_element_type | solution.py:374
  (79 shorter events, 18.5 us)
Async XLA Ops:
  7.2 111.9 %copy-start = (bf16[512,2048]{1,0:T(8,128)(2,1)S(1)}, bf16[512,2048]{1,0:T(8,128)(2,1)}, u32[]{:S(2)}) copy-start(bf16[512,2048]{1,0:T(8,128)(2,1)} %param.27) | copy-start | bytes 6291460
  7.2 137.7 %all-gather.3.cloned.1.call-start = ((), (), s32[]{:S(2)}) async-start(), calls=%async_computation | async-start | bytes 12255232 | tf_op jit(solution)/shard_map/all_gather | solution.py:358
  9.4 156.1 %all-gather.5.cloned.1.call-start = ((), (), s32[]{:S(2)}) async-start(), calls=%async_computation.1 | async-start | bytes 6127616 | tf_op jit(solution)/shard_map/all_gather | solution.py:366
  9.4 4.1 %copy-start.5 = (bf16[1024,2048]{1,0:T(8,128)(2,1)S(1)}, bf16[1024,2048]{1,0:T(8,128)(2,1)}, u32[]{:S(2)}) copy-start(bf16[1024,2048]{1,0:T(8,128)(2,1)} %param.18) | copy-start | bytes 12582916
  13.6 13.0 %copy-start.7 = (bf16[1408,128]{1,0:T(8,128)(2,1)S(1)}, bf16[1408,128]{1,0:T(8,128)(2,1)}, u32[]{:S(2)}) copy-start(bf16[1408,128]{1,0:T(8,128)(2,1)} %param.31) | copy-start | bytes 1081348
  13.6 14.0 %copy-start.13 = (bf16[2048,16]{0,1:T(8,128)(2,1)S(1)}, bf16[2048,16]{0,1:T(8,128)(2,1)}, u32[]{:S(2)}) copy-start(bf16[2048,16]{0,1:T(8,128)(2,1)} %param.22) | copy-start | bytes 196612
  13.6 14.0 %copy-start.14 = (bf16[16,256]{1,0:T(8,128)(2,1)S(1)}, bf16[16,256]{1,0:T(8,128)(2,1)}, u32[]{:S(2)}) copy-start(bf16[16,256]{1,0:T(8,128)(2,1)} %param.23) | copy-start | bytes 24580
  13.6 14.0 %copy-start.15 = (f32[256]{0:T(256)S(1)}, f32[256]{0:T(256)}, u32[]{:S(2)}) copy-start(f32[256]{0:T(256)} %param.24) | copy-start | bytes 3076
  20.9 1.3 copy-start.6
  22.2 21.4 %collective-permute-start = (bf16[3,1024]{1,0:T(4,128)(2,1)S(1)}, bf16[3,1024]{1,0:T(4,128)(2,1)S(1)}, u32[]{:S(2)}, u32[]{:S(2)}) collective-permute-start(bf16[3,1024]{1,0:T(4,128)(2,1)S(1)} %slice_bitcast_fusion.6), channel_id=1, source_target_pairs={{0,2},{2,4},{4,6},{1,3},{3,5},{5,7},{8,10},{10,12},{12,14},{9,11},... | collective-permute-start | bytes 18440 | tf_op jit(solution)/shard_map/ppermute | solution.py:25
  27.6 7.2 %copy-start.10 = (s32[1,16]{1,0:T(1,128)S(1)}, s32[1,16]{1,0:T(1,128)}, u32[]{:S(2)}) copy-start(s32[1,16]{1,0:T(1,128)} %param.33) | copy-start | bytes 196
  27.6 7.2 %copy-start.12 = (s32[1,16]{1,0:T(1,128)S(1)}, s32[1,16]{1,0:T(1,128)}, u32[]{:S(2)}) copy-start(s32[1,16]{1,0:T(1,128)} %param.32) | copy-start | bytes 196
  27.6 7.3 %copy-start.8 = (bf16[4,1024]{1,0:T(4,128)(2,1)S(1)}, bf16[4,1024]{1,0:T(4,128)(2,1)}, u32[]{:S(2)}) copy-start(bf16[4,1024]{1,0:T(4,128)(2,1)} %param.21) | copy-start | bytes 24580
  32.8 10.0 %copy-start.11 = (bf16[512]{0:T(512)(128)(2,1)S(1)}, bf16[512]{0:T(512)(128)(2,1)}, u32[]{:S(2)}) copy-start(bf16[512]{0:T(512)(128)(2,1)} %param.26) | copy-start | bytes 3076
  32.8 10.0 %copy-start.9 = (bf16[2048]{0:T(1024)(128)(2,1)S(1)}, bf16[2048]{0:T(1024)(128)(2,1)}, u32[]{:S(2)}) copy-start(bf16[2048]{0:T(1024)(128)(2,1)} %param.28) | copy-start | bytes 12292
  34.7 63.8 %copy-start.4 = (f32[16,1,64,256]{3,0,1,2:T(8,128)}, f32[16,1,64,256]{3,0,1,2:T(8,128)S(1)}, u32[]{:S(2)}) copy-start(f32[16,1,64,256]{3,0,1,2:T(8,128)S(1)} %fusion.40) | copy-start | bytes 3145732
  51.7 6.1 %copy-start.2 = (f32[16,64,1,1024]{3,1,0,2:T(8,128)}, f32[16,64,1,1024]{3,1,0,2:T(8,128)S(1)}, u32[]{:S(2)}) copy-start(f32[16,64,1,1024]{3,1,0,2:T(8,128)S(1)} %fusion.12) | copy-start | bytes 12582916
  92.4 3.7 %copy-start.3 = (f32[16,64,1,1024]{3,1,0,2:T(8,128)S(1)}, f32[16,64,1,1024]{3,1,0,2:T(8,128)}, u32[]{:S(2)}) copy-start(f32[16,64,1,1024]{3,1,0,2:T(8,128)} %copy-done.2) | copy-start | bytes 12582916
  176.5 10.1 %copy-start.1 = (bf16[512,2048]{1,0:T(8,128)(2,1)S(1)}, bf16[512,2048]{1,0:T(8,128)(2,1)}, u32[]{:S(2)}) copy-start(bf16[512,2048]{1,0:T(8,128)(2,1)} %param.27) | copy-start | bytes 6291460
Sparse Core Ops, SparseCore 0:
  10.2 88.3 all-gather.2
  100.6 58.4 all-gather.4

commit v2 on v1

--- a/solution.py
+++ b/solution.py
@@ -53,33 +53,41 @@
     return lax.fori_loop(0, place, one, state)
 
 
-def partner_kernel(rows, src_ref, dst_ref, send_sem, recv_sem):
+def partner_kernel(rows, pieces, src_ref, dst_ref, send_sem, recv_sem):
     partner = 1 - lax.axis_index("hid")
     barrier = pltpu.get_barrier_semaphore()
     pl.semaphore_signal(
         barrier, inc=1, device_id={"hid": partner}, device_id_type=pl.DeviceIdType.MESH
     )
     pl.semaphore_wait(barrier, 1)
-    start = pl.multiple_of(partner * rows, rows) if rows < src_ref.shape[0] else 0
-    copy = pltpu.make_async_remote_copy(
-        src_ref=src_ref.at[pl.ds(start, rows)],
-        dst_ref=dst_ref,
-        send_sem=send_sem,
-        recv_sem=recv_sem,
-        device_id={"hid": partner},
-        device_id_type=pl.DeviceIdType.MESH,
-    )
-    copy.start()
-    copy.wait()
-
-
-def from_partner(value, rows, kernel_id):
+    start = partner * rows if rows < src_ref.shape[0] else 0
+    share = rows // pieces
+    copies = []
+    for piece in range(pieces):
+        copy = pltpu.make_async_remote_copy(
+            src_ref=src_ref.at[pl.ds(start + piece * share, share)],
+            dst_ref=dst_ref.at[pl.ds(piece * share, share)],
+            send_sem=send_sem.at[piece],
+            recv_sem=recv_sem.at[piece],
+            device_id={"hid": partner},
+            device_id_type=pl.DeviceIdType.MESH,
+        )
+        copy.start()
+        copies.append(copy)
+    for copy in copies:
+        copy.wait()
+
+
+def from_partner(value, rows, kernel_id, pieces=4):
     return pl.pallas_call(
-        functools.partial(partner_kernel, rows),
+        functools.partial(partner_kernel, rows, pieces),
         out_shape=jax.ShapeDtypeStruct((rows,) + value.shape[1:], value.dtype),
         in_specs=[pl.BlockSpec(memory_space=pl.ANY)],
         out_specs=pl.BlockSpec(memory_space=pl.ANY),
-        scratch_shapes=[pltpu.SemaphoreType.DMA, pltpu.SemaphoreType.DMA],
+        scratch_shapes=[
+            pltpu.SemaphoreType.DMA((pieces,)),
+            pltpu.SemaphoreType.DMA((pieces,)),
+        ],
         compiler_params=pltpu.CompilerParams(collective_id=kernel_id, has_side_effects=True),
     )(value)
 

time: 195 us -> 196 us (level)
  no operation moved by 1% of the time
where the time goes in v2:
time: 196 us; the launch traced here: 194 us
  matrix products  77.8 us (40%)
  other arithmetic  44.1 us (22%)
  Pallas kernels  39.2 us (20%)
  between operations  14.4 us (7%)
  local copies, waits for them, and re-layouts  13.5 us (7%)
  starting transfers between devices  4.45 us (2%)
    dot_general x1, matrix products, widen(): return jnp.dot(feed_in, weight_rows, preferred_element_type=jnp.float32)  17.7 us
    pallas_call x1, Pallas kernels, spread_over_seq(): pl.pallas_call(spread_kernel, out_shape=jax.ShapeDtypeStruct((count,) + v...  15.3 us
    pallas_call x2, Pallas kernels, from_partner(): pl.pallas_call(functools.partial(partner_kernel, rows, pieces), out_shape...  12.9 us
    reduce_sum x2, other arithmetic, rms_scaled(): jnp.mean(values * values, axis=-1, keepdims=True) + EPSILON  11.2 us
    dot_general x1, matrix products, on_device(): lax.dot_general(hidden, down_rows, (((1,), (1,)), ((), ())), preferred_el...  10.9 us
    pallas_call x1, Pallas kernels, page_recurrence(): pl.pallas_call(recurrence_kernel, out_shape=(jax.ShapeDtypeStruct(terms.s...  10.9 us
    dot_general x1, matrix products, page_block(): jnp.einsum('phik,phkv->phiv', raised_rows, previous, precision=TOP_PRECIS...  8.04 us
    reshape x1, other arithmetic, on_device(): short_conv(by_page, before, carried, conv_weight)  8.01 us
  transfers between devices with their start and end apart: 3, of which 0 were waited for; matrix products, arithmetic and copies ran while one was open for 60% of the time, Pallas kernels for 18%

profile of v2, /device:TPU:1, one launch (start us, length us, event | category | flops | bytes accessed | tf_op | source)
XLA Modules:
  0.0 193.7 jit_solution(3866227580028718840)
XLA Ops:
  10.3 3.3 %fusion.3 = f32[1024]{0:T(1024)S(1)} fusion(bf16[1024,2048]{1,0:T(8,128)(2,1)} %param.18), kind=kLoop, calls=%fused_computation.10 | loop fusion | flops 6290432 | bytes 4198400 | tf_op jit(solution)/shard_map/reduce_sum | solution.py:198
  13.6 7.3 %convolution_convert_fusion.2 = bf16[1024,1024]{1,0:T(8,128)(2,1)S(1)} fusion(bf16[2048,1024]{1,0:T(8,128)(2,1)} %param.20, bf16[1024,2048]{1,0:T(8,128)(2,1)S(1)} %copy-done.5, f32[2048]{0:T(1024)S(1)} %convert_element_type.151, f32[1024]{0:T(1024)S(1)} %add_rsqrt_fusion.2), kind=kOutput, calls=%fused_computation.48 | convolution fusion | flops 4304404480 | bytes 10498048 | tf_op jit(solution)/shard_map/dot_general | solution.py:297
  22.2 4.4 %collective-permute-start = (bf16[3,1024]{1,0:T(4,128)(2,1)S(1)}, bf16[3,1024]{1,0:T(4,128)(2,1)S(1)}, u32[]{:S(2)}, u32[]{:S(2)}) collective-permute-start(bf16[3,1024]{1,0:T(4,128)(2,1)S(1)} %slice_bitcast_fusion.6), channel_id=1, source_target_pairs={{0,2},{2,4},{4,6},{1,3},{3,5},{5,7},{8,10},{10,12},{12,14},{9,11},... | collective-permute-start | bytes 18440 | tf_op jit(solution)/shard_map/ppermute | solution.py:25
  27.6 5.2 %fusion.29 = f32[1024,256]{1,0:T(8,128)} fusion(bf16[16,256]{1,0:T(8,128)(2,1)S(1)} %copy-done.14, bf16[2048,16]{0,1:T(8,128)(2,1)S(1)} %copy-done.13, f32[256]{0:T(256)S(1)} %copy-done.15, bf16[1024,2048]{1,0:T(8,128)(2,1)} %param.18, f32[2048]{0:T(1024)S(1)} %convert_element_type.151, f32[1024]{0:T(1024)S(1)} %add_rsqrt_fusion.2), kind=kOutput, calls=%fused_computation.54 | convolution fusion | flops 86523904 | bytes 5329920 | tf_op jit(solution)/shard_map/dot_general | solution.py:310
  37.7 4.1 %convert_element_type.154 = f32[16,64,1024]{2,1,0:T(8,128)} convert(bf16[16,64,1024]{2,1,0:T(8,128)(2,1)} %bitcast.137) | non-fusion elementwise | flops 1048576 | bytes 6291456 | tf_op jit(solution)/shard_map/convert_element_type | solution.py:216
  43.7 8.0 %fusion.12 = f32[16,64,1,1024]{3,1,0,2:T(8,128)S(1)} fusion(f32[16,64,1024]{2,1,0:T(8,128)} %convert_element_type.154, f32[16,3,1024]{2,1,0:T(4,128)S(1)} %convert_multiply_fusion.4, f32[1024]{0:T(1024)S(1)} %bitcast.144, f32[1024]{0:T(1024)S(1)} %bitcast.145, f32[1024]{0:T(1024)S(1)} %bitcast.143, f32[1024]{0:T(1024)S(1)} %bitcast.142), kind=kLoop, calls=%fused_computation.25 | loop fusion | flops 10485760 | bytes 8601600 | tf_op jit(solution)/shard_map/reshape | solution.py:303
  51.7 6.1 %fusion.25.terms_ref = f32[16,256,512]{2,1,0:T(8,128)} fusion(f32[16,64,1,1024]{3,1,0,2:T(8,128)S(1)} %fusion.12, f32[16,1,64,256]{3,0,1,2:T(8,128)S(1)} %fusion.40, f32[16,256]{1,0:T(8,128)S(1)} %get-tuple-element.89), kind=kOutput, calls=%fused_computation.46 | convolution fusion | flops 807141376 | bytes 12599296 | tf_op jit(solution)/shard_map/phte,phtb->pheb/dot_general | solution.py:252
  61.3 10.9 %shard_map.175 = (f32[16,256,512]{2,1,0:T(8,128)}, f32[16,256,512]{2,1,0:T(8,128)}) custom-call(f32[16,256,128]{2,1,0:T(8,128)} %broadcast_in_dim.38.decay_ref, f32[16,256,128]{2,1,0:T(8,128)} %broadcast_in_dim.39.carried_ref, f32[16,256,512]{2,1,0:T(8,128)} %fusion.25.terms_ref), custom_call_target="tpu_custom_call" | custom-call | tf_op jit(solution)/shard_map/pallas_call | solution.py:181
  74.0 15.3 %shard_map.176 = bf16[4,257,512]{2,1,0:T(8,128)(2,1)} custom-call(bf16[257,512]{1,0:T(8,128)(2,1)} %fusion.54.src_ref), custom_call_target="tpu_custom_call" | custom-call | tf_op jit(solution)/shard_map/pallas_call | solution.py:146
  89.4 2.3 %slice_bitcast_fusion.3 = bf16[4,1,256,512]{3,2,1,0:T(8,128)(2,1)} fusion(bf16[4,257,512]{2,1,0:T(8,128)(2,1)} %shard_map.176), kind=kLoop, calls=%fused_computation.70 | loop fusion | bytes 2097152 | tf_op jit(solution)/shard_map/while | solution.py:53
  92.4 3.7 %convolution_select_fusion = f32[16,64,64]{2,1,0:T(8,128)S(1)} fusion(f32[16,1,64,256]{3,0,1,2:T(8,128)S(1)} %fusion.40, pred[64,64]{1,0:T(8,128)(4,1)S(1)} %iota_compare_fusion.1, f32[16,64,1,1024]{3,1,0,2:T(8,128)} %copy-done.2), kind=kOutput, calls=%fused_computation.51 | convolution fusion | flops 103874560 | bytes 4464640 | tf_op jit(solution)/shard_map/phik,phjk->phij/dot_general | solution.py:245
  96.1 2.4 %fusion.26 = f32[16,64,512]{2,1,0:T(8,128)} fusion(f32[16,64,64]{2,1,0:T(8,128)S(1)} %convolution_select_fusion, f32[16,64,1,1024]{3,1,0,2:T(8,128)S(1)} %copy-done.3), kind=kOutput, calls=%fused_computation.47 | convolution fusion | flops 201326592 | bytes 4718592 | tf_op jit(solution)/shard_map/phij,phjv->phiv/dot_general | solution.py:249
  98.5 8.0 %fusion.42 = f32[16,64,512]{2,1,0:T(8,128)} fusion(f32[16,256,512]{2,1,0:T(8,128)} %get-tuple-element.49, f32[16,1,64,256]{3,0,1,2:T(8,128)S(1)} %fusion.40, f32[16,64,1,1024]{3,1,0,2:T(8,128)S(1)} %copy-done.3), kind=kOutput, calls=%fused_computation.73 | convolution fusion | flops 806617088 | bytes 12582912 | tf_op jit(solution)/shard_map/phik,phkv->phiv/dot_general | solution.py:264
  106.8 5.9 %multiply_reduce_fusion = (f32[16,64]{1,0:T(8,128)S(1)}, f32[16,1,64,512]{3,2,0,1:T(8,128)}) fusion(f32[16,1,64,256]{3,0,1,2:T(8,128)} %copy-done.4, f32[16,256]{1,0:T(8,128)S(1)} %get-tuple-element.88, f32[16]{0:T(128)S(1)} %reduce.2, f32[16,64,1,1024]{3,1,0,2:T(8,128)} %copy-done.2, f32[1,256,512]{2,1,0:T(8,128)S(1)} %get-tuple-element.51, ...), kind=kOutput, calls=%fused_computation.45 | convolution fusion | flops 809237504 | bytes 8933440 | tf_op jit(solution)/shard_map/dlof,lfg->dlog/dot_general | solution.py:336
  112.9 6.2 %fusion.24 = bf16[1024,512]{1,0:T(8,128)(2,1)S(1)} fusion(f32[16,1,64,512]{3,2,0,1:T(8,128)} %get-tuple-element.95, f32[512]{0:T(512)S(1)} %convert_element_type.164, f32[1024]{0:T(1024)S(1)} %rsqrt.29, bf16[2048,512]{1,0:T(8,128)(2,1)} %param.25, bf16[1024,2048]{1,0:T(8,128)(2,1)} %param.18, f32[2048]{0:T(1024)S(1)} %convert_element_type.151, ...), kind=kOutput, calls=%fused_computation.44 | convolution fusion | flops 2160066560 | bytes 9455616 | tf_op jit(solution)/shard_map/dot_general | solution.py:344
  119.1 4.4 %convolution_convert_fusion.1.src_ref = bf16[1024,2048]{1,0:T(8,128)(2,1)} fusion(bf16[1024,512]{1,0:T(8,128)(2,1)S(1)} %fusion.24, bf16[512,2048]{1,0:T(8,128)(2,1)S(1)} %copy-done), kind=kOutput, calls=%fused_computation.37 | convolution fusion | flops 2149580800 | bytes 7340032 | tf_op jit(solution)/shard_map/dot_general | solution.py:350
  123.4 8.4 %shard_map.177 = bf16[1024,2048]{1,0:T(8,128)(2,1)} custom-call(bf16[1024,2048]{1,0:T(8,128)(2,1)} %convolution_convert_fusion.1.src_ref), custom_call_target="tpu_custom_call" | custom-call | tf_op jit(solution)/shard_map/pallas_call | solution.py:82
  131.8 7.9 %fusion = (f32[1024]{0:T(1024)S(1)}, bf16[1024,2048]{1,0:T(8,128)(2,1)}) fusion(bf16[1024,2048]{1,0:T(8,128)(2,1)} %shard_map.177, bf16[1024,2048]{1,0:T(8,128)(2,1)} %convolution_convert_fusion.1.src_ref, bf16[1024,2048]{1,0:T(8,128)(2,1)} %param.18), kind=kLoop, calls=%fused_computation.7 | loop fusion | flops 18873344 | bytes 16781312 | tf_op jit(solution)/shard_map/reduce_sum | solution.py:198
  139.7 5.4 %fusion.16 = bf16[16,1,256,512]{3,2,1,0:T(8,128)(2,1)} fusion(f32[16,256,512]{2,1,0:T(8,128)} %get-tuple-element.50, f32[256,512]{1,0:T(8,128)S(1)} %bitcast.134, f32[16,256]{1,0:T(8,128)S(1)} %bitcast_multiply_fusion.5), kind=kLoop, calls=%fused_computation.29 | loop fusion | flops 6291456 | bytes 13123584
  145.1 17.7 %fusion.17 = f32[1024,2816]{1,0:T(8,128)S(1)} fusion(bf16[2048,2816]{1,0:T(8,128)(2,1)} %all-gather.3.cloned.1.call-done, bf16[1024,2048]{1,0:T(8,128)(2,1)} %get-tuple-element.87, f32[2048]{0:T(1024)S(1)} %convert_element_type.172, f32[1024]{0:T(1024)S(1)} %add_rsqrt_fusion.1), kind=kOutput, calls=%fused_computation.30 | convolution fusion | flops 11819548672 | bytes 27275264 | tf_op jit(solution)/shard_map/dot_general | solution.py:362
  162.8 2.9 %fusion.7 = bf16[1024,1408]{1,0:T(8,128)(2,1)} fusion(f32[1024,2816]{1,0:T(8,128)S(1)} %fusion.17), kind=kLoop, calls=%fused_computation.18 | loop fusion | flops 8650752 | bytes 14417920 | tf_op jit(solution)/shard_map/convert_element_type | solution.py:372
  165.8 10.9 %convolution_convert_fusion.src_ref = bf16[1024,2048]{1,0:T(8,128)(2,1)} fusion(bf16[1024,1408]{1,0:T(8,128)(2,1)} %fusion.7, bf16[2048,1408]{1,0:T(8,128)(2,1)} %all-gather.5.cloned.1.call-done), kind=kOutput, calls=%fused_computation.36 | convolution fusion | flops 5907677184 | bytes 12845056 | tf_op jit(solution)/shard_map/dot_general | solution.py:375
  176.7 4.6 %shard_map.178 = bf16[512,2048]{1,0:T(8,128)(2,1)} custom-call(bf16[1024,2048]{1,0:T(8,128)(2,1)} %convolution_convert_fusion.src_ref), custom_call_target="tpu_custom_call" | custom-call | tf_op jit(solution)/shard_map/pallas_call | solution.py:82
  181.3 5.6 %add_convert_fusion.1 = bf16[512,2048]{1,0:T(8,128)(2,1)} fusion(bf16[512,2048]{1,0:T(8,128)(2,1)} %shard_map.178, bf16[1024,2048]{1,0:T(8,128)(2,1)} %convolution_convert_fusion.src_ref, s32[]{:T(128)S(6)} %select_n.32, bf16[1024,2048]{1,0:T(8,128)(2,1)} %get-tuple-element.87), kind=kLoop, calls=%fused_computation.33 | loop fusion | flops 6291456 | bytes 8388612 | tf_op jit(solution)/shard_map/convert_element_type | solution.py:382
  (79 shorter events, 18.5 us)
Async XLA Ops:
  7.2 111.9 %copy-start = (bf16[512,2048]{1,0:T(8,128)(2,1)S(1)}, bf16[512,2048]{1,0:T(8,128)(2,1)}, u32[]{:S(2)}) copy-start(bf16[512,2048]{1,0:T(8,128)(2,1)} %param.27) | copy-start | bytes 6291460
  7.2 137.9 %all-gather.3.cloned.1.call-start = ((), (), s32[]{:S(2)}) async-start(), calls=%async_computation | async-start | bytes 12255232 | tf_op jit(solution)/shard_map/all_gather | solution.py:366
  9.4 156.4 %all-gather.5.cloned.1.call-start = ((), (), s32[]{:S(2)}) async-start(), calls=%async_computation.1 | async-start | bytes 6127616 | tf_op jit(solution)/shard_map/all_gather | solution.py:374
  9.4 4.1 %copy-start.5 = (bf16[1024,2048]{1,0:T(8,128)(2,1)S(1)}, bf16[1024,2048]{1,0:T(8,128)(2,1)}, u32[]{:S(2)}) copy-start(bf16[1024,2048]{1,0:T(8,128)(2,1)} %param.18) | copy-start | bytes 12582916
  13.6 13.0 %copy-start.7 = (bf16[1408,128]{1,0:T(8,128)(2,1)S(1)}, bf16[1408,128]{1,0:T(8,128)(2,1)}, u32[]{:S(2)}) copy-start(bf16[1408,128]{1,0:T(8,128)(2,1)} %param.31) | copy-start | bytes 1081348
  13.6 14.0 %copy-start.13 = (bf16[2048,16]{0,1:T(8,128)(2,1)S(1)}, bf16[2048,16]{0,1:T(8,128)(2,1)}, u32[]{:S(2)}) copy-start(bf16[2048,16]{0,1:T(8,128)(2,1)} %param.22) | copy-start | bytes 196612
  13.6 14.0 %copy-start.14 = (bf16[16,256]{1,0:T(8,128)(2,1)S(1)}, bf16[16,256]{1,0:T(8,128)(2,1)}, u32[]{:S(2)}) copy-start(bf16[16,256]{1,0:T(8,128)(2,1)} %param.23) | copy-start | bytes 24580
  13.6 14.0 %copy-start.15 = (f32[256]{0:T(256)S(1)}, f32[256]{0:T(256)}, u32[]{:S(2)}) copy-start(f32[256]{0:T(256)} %param.24) | copy-start | bytes 3076
  20.9 1.3 copy-start.6
  22.2 21.4 %collective-permute-start = (bf16[3,1024]{1,0:T(4,128)(2,1)S(1)}, bf16[3,1024]{1,0:T(4,128)(2,1)S(1)}, u32[]{:S(2)}, u32[]{:S(2)}) collective-permute-start(bf16[3,1024]{1,0:T(4,128)(2,1)S(1)} %slice_bitcast_fusion.6), channel_id=1, source_target_pairs={{0,2},{2,4},{4,6},{1,3},{3,5},{5,7},{8,10},{10,12},{12,14},{9,11},... | collective-permute-start | bytes 18440 | tf_op jit(solution)/shard_map/ppermute | solution.py:25
  27.6 7.2 %copy-start.10 = (s32[1,16]{1,0:T(1,128)S(1)}, s32[1,16]{1,0:T(1,128)}, u32[]{:S(2)}) copy-start(s32[1,16]{1,0:T(1,128)} %param.33) | copy-start | bytes 196
  27.6 7.2 %copy-start.12 = (s32[1,16]{1,0:T(1,128)S(1)}, s32[1,16]{1,0:T(1,128)}, u32[]{:S(2)}) copy-start(s32[1,16]{1,0:T(1,128)} %param.32) | copy-start | bytes 196
  27.6 7.3 %copy-start.8 = (bf16[4,1024]{1,0:T(4,128)(2,1)S(1)}, bf16[4,1024]{1,0:T(4,128)(2,1)}, u32[]{:S(2)}) copy-start(bf16[4,1024]{1,0:T(4,128)(2,1)} %param.21) | copy-start | bytes 24580
  32.8 10.0 %copy-start.11 = (bf16[512]{0:T(512)(128)(2,1)S(1)}, bf16[512]{0:T(512)(128)(2,1)}, u32[]{:S(2)}) copy-start(bf16[512]{0:T(512)(128)(2,1)} %param.26) | copy-start | bytes 3076
  32.8 10.0 %copy-start.9 = (bf16[2048]{0:T(1024)(128)(2,1)S(1)}, bf16[2048]{0:T(1024)(128)(2,1)}, u32[]{:S(2)}) copy-start(bf16[2048]{0:T(1024)(128)(2,1)} %param.28) | copy-start | bytes 12292
  34.7 63.8 %copy-start.4 = (f32[16,1,64,256]{3,0,1,2:T(8,128)}, f32[16,1,64,256]{3,0,1,2:T(8,128)S(1)}, u32[]{:S(2)}) copy-start(f32[16,1,64,256]{3,0,1,2:T(8,128)S(1)} %fusion.40) | copy-start | bytes 3145732
  51.7 6.1 %copy-start.2 = (f32[16,64,1,1024]{3,1,0,2:T(8,128)}, f32[16,64,1,1024]{3,1,0,2:T(8,128)S(1)}, u32[]{:S(2)}) copy-start(f32[16,64,1,1024]{3,1,0,2:T(8,128)S(1)} %fusion.12) | copy-start | bytes 12582916
  92.4 3.7 %copy-start.3 = (f32[16,64,1,1024]{3,1,0,2:T(8,128)S(1)}, f32[16,64,1,1024]{3,1,0,2:T(8,128)}, u32[]{:S(2)}) copy-start(f32[16,64,1,1024]{3,1,0,2:T(8,128)} %copy-done.2) | copy-start | bytes 12582916
  176.7 10.2 %copy-start.1 = (bf16[512,2048]{1,0:T(8,128)(2,1)S(1)}, bf16[512,2048]{1,0:T(8,128)(2,1)}, u32[]{:S(2)}) copy-start(bf16[512,2048]{1,0:T(8,128)(2,1)} %param.27) | copy-start | bytes 6291460
Sparse Core Ops, SparseCore 0:
  10.2 88.3 all-gather.2
  100.6 58.4 all-gather.4

commit v3 on v1

--- a/solution.py
+++ b/solution.py
@@ -148,10 +148,12 @@
     )(value)
 
 
-def recurrence_kernel(decay_ref, carried_ref, terms_ref, out_ref, previous_ref, state_ref):
+def recurrence_kernel(decay_ref, carried_ref, terms_ref, raised_ref, out_ref, inter_ref, state_ref):
     step = pl.program_id(0)
     chunk = terms_ref.shape[0]
     reach = terms_ref.shape[-1] // decay_ref.shape[-1]
+    heads = raised_ref.shape[1]
+    keys = raised_ref.shape[-1]
 
     @pl.when(step == 0)
     def _():
@@ -159,28 +161,40 @@
 
     for page in range(chunk):
         kept = jnp.concatenate([carried_ref[page]] * reach, axis=-1) * state_ref[...]
-        previous_ref[page] = kept
+        for head in range(heads):
+            inter_ref[page, head] = jnp.dot(
+                raised_ref[page, head],
+                kept[head * keys : (head + 1) * keys],
+                preferred_element_type=jnp.float32,
+                precision=lax.Precision.HIGHEST,
+            )
         state = jnp.concatenate([decay_ref[page]] * reach, axis=-1) * kept + terms_ref[page]
         state_ref[...] = state
         out_ref[page] = state
 
 
-def page_recurrence(decay, carried, terms, chunk=4):
+def page_recurrence(decay, carried, terms, raised, chunk=4):
     page_count, rows, width = terms.shape
     lanes = decay.shape[-1]
+    heads, length = raised.shape[1], raised.shape[2]
     block = pl.BlockSpec((chunk, rows, width), lambda p: (p, 0, 0))
     flags = pl.BlockSpec((chunk, rows, lanes), lambda p: (p, 0, 0))
     return pl.pallas_call(
         recurrence_kernel,
         out_shape=(
             jax.ShapeDtypeStruct(terms.shape, terms.dtype),
-            jax.ShapeDtypeStruct(terms.shape, terms.dtype),
+            jax.ShapeDtypeStruct((page_count, heads, length, width), jnp.float32),
         ),
         grid=(page_count // chunk,),
-        in_specs=[flags, flags, block],
-        out_specs=(block, block),
+        in_specs=[
+            flags,
+            flags,
+            block,
+            pl.BlockSpec((chunk,) + raised.shape[1:], lambda p: (p, 0, 0, 0)),
+        ],
+        out_specs=(block, pl.BlockSpec((chunk, heads, length, width), lambda p: (p, 0, 0, 0))),
         scratch_shapes=[pltpu.VMEM((rows, width), jnp.float32)],
-    )(decay, carried, terms)
+    )(decay, carried, terms, raised)
 
 
 def rms_scaled(values, scale_gain):
@@ -246,16 +260,14 @@
     )
     lanes = 128
     rows = closing_sum.shape[1] * closing_sum.shape[2]
-    memories, previous = page_recurrence(
+    memories, inter_output = page_recurrence(
         jnp.broadcast_to(jnp.exp(closing_sum).reshape(page_count, rows, 1), (page_count, rows, lanes)),
         jnp.broadcast_to(carried[:, None, None], (page_count, rows, lanes)),
         page_terms.reshape(page_count, rows, page_terms.shape[-1]),
+        raised_rows,
     )
     memories = memories.reshape(page_terms.shape)
-    previous = previous.reshape(page_terms.shape)
-    layer_output = layer_output + jnp.einsum(
-        "phik,phkv->phiv", raised_rows, previous, precision=TOP_PRECISION
-    )
+    layer_output = layer_output + inter_output
     return memories[-1], layer_output, memories
 
 

time: 195 us -> 189 us (0.969)
  matrix products: 77.8 us -> 69.8 us
  other arithmetic: 43.9 us -> 45.9 us
    dot_general x1 -> x0, matrix products: 8.04 us -> none  [page_block(): jnp.einsum('phik,phkv->phiv', raised_rows, previous, precision=TOP_PRECIS...]
    mul x0 -> x1, other arithmetic: none -> 2.35 us  [page_block(): raised_rows = query_rows * jnp.exp(decay_sum)]
  transfers between devices with their start and end apart: 3 -> 3, of which waited for: 0 -> 1; matrix products, arithmetic and copies ran while one was open for 60% -> 58% of each run, Pallas kernels for 18% -> 19%
where the time goes in v3:
time: 189 us; the launch traced here: 187 us
  matrix products  69.8 us (37%)
  other arithmetic  45.9 us (24%)
  Pallas kernels  39.8 us (21%)
  between operations  14.5 us (8%)
  local copies, waits for them, and re-layouts  12.2 us (6%)
  starting transfers between devices  4.45 us (2%)
    dot_general x1, matrix products, widen(): return jnp.dot(feed_in, weight_rows, preferred_element_type=jnp.float32)  17.7 us
    pallas_call x1, Pallas kernels, spread_over_seq(): pl.pallas_call(spread_kernel, out_shape=jax.ShapeDtypeStruct((count,) + v...  15.4 us
    pallas_call x2, Pallas kernels, from_partner(): pl.pallas_call(functools.partial(partner_kernel, rows), out_shape=jax.Sha...  13.1 us
    pallas_call x1, Pallas kernels, page_recurrence(): pl.pallas_call(recurrence_kernel, out_shape=(jax.ShapeDtypeStruct(terms.s...  11.2 us
    dot_general x1, matrix products, on_device(): lax.dot_general(hidden, down_rows, (((1,), (1,)), ((), ())), preferred_el...  10.9 us
    reduce_sum x2, other arithmetic, rms_scaled(): jnp.mean(values * values, axis=-1, keepdims=True) + EPSILON  10.8 us
    reshape x1, other arithmetic, on_device(): short_conv(by_page, before, carried, conv_weight)  8 us
    dot_general x1, matrix products, on_device(): jnp.dot(normed, project_weight, preferred_element_type=jnp.float32)  7.26 us
  transfers between devices with their start and end apart: 3, of which 1 were waited for; matrix products, arithmetic and copies ran while one was open for 58% of the time, Pallas kernels for 19%

profile of v3, /device:TPU:1, one launch (start us, length us, event | category | flops | bytes accessed | tf_op | source)
XLA Modules:
  0.0 187.3 jit_solution(7415205503488581378)
XLA Ops:
  7.2 2.1 %pad_maximum_fusion.1 = bf16[128,2816]{1,0:T(8,128)(2,1)} fusion(bf16[128,1408]{1,0:T(8,128)(2,1)} %param.30, bf16[128,1408]{1,0:T(8,128)(2,1)} %param.29), kind=kLoop, calls=%fused_computation.80 | loop fusion | flops 1441792 | bytes 1441792 | tf_op jit(solution)/shard_map/concatenate | solution.py:371
  10.3 3.3 %fusion.3 = f32[1024]{0:T(1024)S(1)} fusion(bf16[1024,2048]{1,0:T(8,128)(2,1)} %param.18), kind=kLoop, calls=%fused_computation.10 | loop fusion | flops 6290432 | bytes 4198400 | tf_op jit(solution)/shard_map/reduce_sum | solution.py:204
  13.6 7.3 %convolution_convert_fusion.2 = bf16[1024,1024]{1,0:T(8,128)(2,1)S(1)} fusion(bf16[2048,1024]{1,0:T(8,128)(2,1)} %param.20, bf16[1024,2048]{1,0:T(8,128)(2,1)S(1)} %copy-done.5, f32[2048]{0:T(1024)S(1)} %convert_element_type.151, f32[1024]{0:T(1024)S(1)} %add_rsqrt_fusion.2), kind=kOutput, calls=%fused_computation.49 | convolution fusion | flops 4304404480 | bytes 10498048 | tf_op jit(solution)/shard_map/dot_general | solution.py:301
  22.2 4.4 %collective-permute-start = (bf16[3,1024]{1,0:T(4,128)(2,1)S(1)}, bf16[3,1024]{1,0:T(4,128)(2,1)S(1)}, u32[]{:S(2)}, u32[]{:S(2)}) collective-permute-start(bf16[3,1024]{1,0:T(4,128)(2,1)S(1)} %slice_bitcast_fusion.6), channel_id=1, source_target_pairs={{0,2},{2,4},{4,6},{1,3},{3,5},{5,7},{8,10},{10,12},{12,14},{9,11},... | collective-permute-start | bytes 18440 | tf_op jit(solution)/shard_map/ppermute | solution.py:25
  27.6 5.2 %fusion.29 = f32[1024,256]{1,0:T(8,128)} fusion(bf16[16,256]{1,0:T(8,128)(2,1)S(1)} %copy-done.15, bf16[2048,16]{0,1:T(8,128)(2,1)S(1)} %copy-done.14, f32[256]{0:T(256)S(1)} %copy-done.16, bf16[1024,2048]{1,0:T(8,128)(2,1)} %param.18, f32[2048]{0:T(1024)S(1)} %convert_element_type.151, f32[1024]{0:T(1024)S(1)} %add_rsqrt_fusion.2), kind=kOutput, calls=%fused_computation.55 | convolution fusion | flops 86523904 | bytes 5329920 | tf_op jit(solution)/shard_map/dot_general | solution.py:314
  37.7 4.1 %convert_element_type.154 = f32[16,64,1024]{2,1,0:T(8,128)} convert(bf16[16,64,1024]{2,1,0:T(8,128)(2,1)} %bitcast.140) | non-fusion elementwise | flops 1048576 | bytes 6291456 | tf_op jit(solution)/shard_map/convert_element_type | solution.py:222
  43.7 8.0 %fusion.12 = f32[16,64,1,1024]{3,1,0,2:T(8,128)S(1)} fusion(f32[16,64,1024]{2,1,0:T(8,128)} %convert_element_type.154, f32[16,3,1024]{2,1,0:T(4,128)S(1)} %convert_multiply_fusion.4, f32[1024]{0:T(1024)S(1)} %bitcast.147, f32[1024]{0:T(1024)S(1)} %bitcast.148, f32[1024]{0:T(1024)S(1)} %bitcast.146, f32[1024]{0:T(1024)S(1)} %bitcast.145), kind=kLoop, calls=%fused_computation.25 | loop fusion | flops 10485760 | bytes 8601600 | tf_op jit(solution)/shard_map/reshape | solution.py:307
  51.7 2.4 %bitcast_multiply_fusion.1.raised_ref = f32[16,1,64,256]{3,2,1,0:T(8,128)} fusion(f32[16,1,64,256]{3,0,1,2:T(8,128)S(1)} %fusion.42, f32[16,64,1,1024]{3,1,0,2:T(8,128)S(1)} %fusion.12), kind=kLoop, calls=%fused_computation.61 | loop fusion | flops 1310720 | bytes 3145728 | tf_op jit(solution)/shard_map/mul | solution.py:249
  54.1 6.2 %fusion.25.terms_ref = f32[16,256,512]{2,1,0:T(8,128)} fusion(f32[16,64,1,1024]{3,1,0,2:T(8,128)S(1)} %fusion.12, f32[16,1,64,256]{3,0,1,2:T(8,128)S(1)} %fusion.42, f32[16,256]{1,0:T(8,128)S(1)} %get-tuple-element.89), kind=kOutput, calls=%fused_computation.47 | convolution fusion | flops 807141376 | bytes 12599296 | tf_op jit(solution)/shard_map/phte,phtb->pheb/dot_general | solution.py:258
  63.7 11.2 %shard_map.175 = (f32[16,256,512]{2,1,0:T(8,128)}, f32[16,1,64,512]{3,2,1,0:T(8,128)}) custom-call(f32[16,256,128]{2,1,0:T(8,128)} %broadcast_in_dim.38.decay_ref, f32[16,256,128]{2,1,0:T(8,128)} %broadcast_in_dim.39.carried_ref, f32[16,256,512]{2,1,0:T(8,128)} %fusion.25.terms_ref, f32[16,1,64,256]{3,2,1,0:T(8,128)} %bitcast_multiply_fusion.1.raised_ref), custom_call_target="tpu_custom_call" | custom-call | tf_op jit(solution)/shard_map/pallas_call | solution.py:182
  76.7 15.4 %shard_map.176 = bf16[4,257,512]{2,1,0:T(8,128)(2,1)} custom-call(bf16[257,512]{1,0:T(8,128)(2,1)} %fusion.52.src_ref), custom_call_target="tpu_custom_call" | custom-call | tf_op jit(solution)/shard_map/pallas_call | solution.py:138
  92.9 3.7 %convolution_select_fusion = f32[16,64,64]{2,1,0:T(8,128)S(1)} fusion(f32[16,1,64,256]{3,0,1,2:T(8,128)S(1)} %fusion.42, pred[64,64]{1,0:T(8,128)(4,1)S(1)} %iota_compare_fusion.1, f32[16,64,1,1024]{3,1,0,2:T(8,128)} %copy-done.2), kind=kOutput, calls=%fused_computation.52 | convolution fusion | flops 103874560 | bytes 4464640 | tf_op jit(solution)/shard_map/phik,phjk->phij/dot_general | solution.py:251
  97.6 2.4 %fusion.26 = f32[16,64,512]{2,1,0:T(8,128)} fusion(f32[16,64,64]{2,1,0:T(8,128)S(1)} %convolution_select_fusion, f32[16,64,1,1024]{3,1,0,2:T(8,128)S(1)} %copy-done.3), kind=kOutput, calls=%fused_computation.48 | convolution fusion | flops 201326592 | bytes 4718592 | tf_op jit(solution)/shard_map/phij,phjv->phiv/dot_general | solution.py:255
  100.3 5.9 %multiply_reduce_fusion = (f32[16,64]{1,0:T(8,128)S(1)}, f32[16,1,64,512]{3,2,1,0:T(8,128)}) fusion(f32[16,1,64,256]{3,0,1,2:T(8,128)} %copy-done.4, f32[16,256]{1,0:T(8,128)S(1)} %get-tuple-element.88, f32[16]{0:T(128)S(1)} %reduce.2, f32[16,64,1,1024]{3,1,0,2:T(8,128)} %copy-done.2, f32[1,256,512]{2,1,0:T(8,128)S(1)} %get-tuple-element.51, ...), kind=kOutput, calls=%fused_computation.46 | convolution fusion | flops 809237504 | bytes 8933440 | tf_op jit(solution)/shard_map/dlof,lfg->dlog/dot_general | solution.py:340
  106.3 6.2 %fusion.24 = bf16[1024,512]{1,0:T(8,128)(2,1)S(1)} fusion(f32[16,1,64,512]{3,2,1,0:T(8,128)} %get-tuple-element.95, f32[512]{0:T(512)S(1)} %convert_element_type.164, f32[1024]{0:T(1024)S(1)} %rsqrt.29, bf16[2048,512]{1,0:T(8,128)(2,1)} %param.25, bf16[1024,2048]{1,0:T(8,128)(2,1)} %param.18, f32[2048]{0:T(1024)S(1)} %convert_element_type.151, ...), kind=kOutput, calls=%fused_computation.44 | convolution fusion | flops 2160066560 | bytes 9455616 | tf_op jit(solution)/shard_map/dot_general | solution.py:348
  112.5 4.4 %convolution_convert_fusion.1.src_ref = bf16[1024,2048]{1,0:T(8,128)(2,1)} fusion(bf16[1024,512]{1,0:T(8,128)(2,1)S(1)} %fusion.24, bf16[512,2048]{1,0:T(8,128)(2,1)S(1)} %copy-done), kind=kOutput, calls=%fused_computation.37 | convolution fusion | flops 2149580800 | bytes 7340032 | tf_op jit(solution)/shard_map/dot_general | solution.py:354
  116.8 8.3 %shard_map.177 = bf16[1024,2048]{1,0:T(8,128)(2,1)} custom-call(bf16[1024,2048]{1,0:T(8,128)(2,1)} %convolution_convert_fusion.1.src_ref), custom_call_target="tpu_custom_call" | custom-call | tf_op jit(solution)/shard_map/pallas_call | solution.py:77
  125.1 7.5 %fusion = (f32[1024]{0:T(1024)S(1)}, bf16[1024,2048]{1,0:T(8,128)(2,1)}) fusion(bf16[1024,2048]{1,0:T(8,128)(2,1)} %shard_map.177, bf16[1024,2048]{1,0:T(8,128)(2,1)} %convolution_convert_fusion.1.src_ref, bf16[1024,2048]{1,0:T(8,128)(2,1)} %param.18), kind=kLoop, calls=%fused_computation.7 | loop fusion | flops 18873344 | bytes 16781312 | tf_op jit(solution)/shard_map/reduce_sum | solution.py:204
  132.7 5.3 %fusion.16 = bf16[16,1,256,512]{3,2,1,0:T(8,128)(2,1)} fusion(f32[16,256,512]{2,1,0:T(8,128)} %get-tuple-element.50, f32[256,512]{1,0:T(8,128)S(1)} %bitcast.137, f32[16,256]{1,0:T(8,128)S(1)} %bitcast_multiply_fusion.6), kind=kLoop, calls=%fused_computation.29 | loop fusion | flops 6291456 | bytes 13123584
  138.0 17.7 %fusion.17 = f32[1024,2816]{1,0:T(8,128)S(1)} fusion(bf16[2048,2816]{1,0:T(8,128)(2,1)} %all-gather.3.cloned.1.call-done, bf16[1024,2048]{1,0:T(8,128)(2,1)} %get-tuple-element.87, f32[2048]{0:T(1024)S(1)} %convert_element_type.172, f32[1024]{0:T(1024)S(1)} %add_rsqrt_fusion.1), kind=kOutput, calls=%fused_computation.30 | convolution fusion | flops 11819548672 | bytes 27275264 | tf_op jit(solution)/shard_map/dot_general | solution.py:366
  155.7 2.9 %fusion.7 = bf16[1024,1408]{1,0:T(8,128)(2,1)} fusion(f32[1024,2816]{1,0:T(8,128)S(1)} %fusion.17), kind=kLoop, calls=%fused_computation.18 | loop fusion | flops 8650752 | bytes 14417920 | tf_op jit(solution)/shard_map/convert_element_type | solution.py:376
  159.1 10.9 %convolution_convert_fusion.src_ref = bf16[1024,2048]{1,0:T(8,128)(2,1)} fusion(bf16[1024,1408]{1,0:T(8,128)(2,1)} %fusion.7, bf16[2048,1408]{1,0:T(8,128)(2,1)} %all-gather.5.cloned.1.call-done), kind=kOutput, calls=%fused_computation.36 | convolution fusion | flops 5907677184 | bytes 12845056 | tf_op jit(solution)/shard_map/dot_general | solution.py:379
  170.1 4.8 %shard_map.178 = bf16[512,2048]{1,0:T(8,128)(2,1)} custom-call(bf16[1024,2048]{1,0:T(8,128)(2,1)} %convolution_convert_fusion.src_ref), custom_call_target="tpu_custom_call" | custom-call | tf_op jit(solution)/shard_map/pallas_call | solution.py:77
  174.9 5.6 %add_convert_fusion.1 = bf16[512,2048]{1,0:T(8,128)(2,1)} fusion(bf16[512,2048]{1,0:T(8,128)(2,1)} %shard_map.178, bf16[1024,2048]{1,0:T(8,128)(2,1)} %convolution_convert_fusion.src_ref, s32[]{:T(128)S(6)} %select_n.32, bf16[1024,2048]{1,0:T(8,128)(2,1)} %get-tuple-element.87), kind=kLoop, calls=%fused_computation.33 | loop fusion | flops 6291456 | bytes 8388612 | tf_op jit(solution)/shard_map/convert_element_type | solution.py:386
  (81 shorter events, 17.7 us)
Async XLA Ops:
  7.2 105.3 %copy-start = (bf16[512,2048]{1,0:T(8,128)(2,1)S(1)}, bf16[512,2048]{1,0:T(8,128)(2,1)}, u32[]{:S(2)}) copy-start(bf16[512,2048]{1,0:T(8,128)(2,1)} %param.27) | copy-start | bytes 6291460
  7.2 130.8 %all-gather.3.cloned.1.call-start = ((), (), s32[]{:S(2)}) async-start(), calls=%async_computation | async-start | bytes 12255232 | tf_op jit(solution)/shard_map/all_gather | solution.py:370
  9.4 149.7 %all-gather.5.cloned.1.call-start = ((), (), s32[]{:S(2)}) async-start(), calls=%async_computation.1 | async-start | bytes 6127616 | tf_op jit(solution)/shard_map/all_gather | solution.py:378
  9.4 4.1 %copy-start.5 = (bf16[1024,2048]{1,0:T(8,128)(2,1)S(1)}, bf16[1024,2048]{1,0:T(8,128)(2,1)}, u32[]{:S(2)}) copy-start(bf16[1024,2048]{1,0:T(8,128)(2,1)} %param.18) | copy-start | bytes 12582916
  13.6 13.0 %copy-start.8 = (bf16[1408,128]{1,0:T(8,128)(2,1)S(1)}, bf16[1408,128]{1,0:T(8,128)(2,1)}, u32[]{:S(2)}) copy-start(bf16[1408,128]{1,0:T(8,128)(2,1)} %param.31) | copy-start | bytes 1081348
  13.6 14.0 %copy-start.14 = (bf16[2048,16]{0,1:T(8,128)(2,1)S(1)}, bf16[2048,16]{0,1:T(8,128)(2,1)}, u32[]{:S(2)}) copy-start(bf16[2048,16]{0,1:T(8,128)(2,1)} %param.22) | copy-start | bytes 196612
  13.6 14.0 %copy-start.15 = (bf16[16,256]{1,0:T(8,128)(2,1)S(1)}, bf16[16,256]{1,0:T(8,128)(2,1)}, u32[]{:S(2)}) copy-start(bf16[16,256]{1,0:T(8,128)(2,1)} %param.23) | copy-start | bytes 24580
  13.6 14.0 %copy-start.16 = (f32[256]{0:T(256)S(1)}, f32[256]{0:T(256)}, u32[]{:S(2)}) copy-start(f32[256]{0:T(256)} %param.24) | copy-start | bytes 3076
  20.9 1.3 copy-start.7
  22.2 21.3 %collective-permute-start = (bf16[3,1024]{1,0:T(4,128)(2,1)S(1)}, bf16[3,1024]{1,0:T(4,128)(2,1)S(1)}, u32[]{:S(2)}, u32[]{:S(2)}) collective-permute-start(bf16[3,1024]{1,0:T(4,128)(2,1)S(1)} %slice_bitcast_fusion.6), channel_id=1, source_target_pairs={{0,2},{2,4},{4,6},{1,3},{3,5},{5,7},{8,10},{10,12},{12,14},{9,11},... | collective-permute-start | bytes 18440 | tf_op jit(solution)/shard_map/ppermute | solution.py:25
  27.6 7.2 %copy-start.11 = (s32[1,16]{1,0:T(1,128)S(1)}, s32[1,16]{1,0:T(1,128)}, u32[]{:S(2)}) copy-start(s32[1,16]{1,0:T(1,128)} %param.33) | copy-start | bytes 196
  27.6 7.2 %copy-start.13 = (s32[1,16]{1,0:T(1,128)S(1)}, s32[1,16]{1,0:T(1,128)}, u32[]{:S(2)}) copy-start(s32[1,16]{1,0:T(1,128)} %param.32) | copy-start | bytes 196
  27.6 7.3 %copy-start.9 = (bf16[4,1024]{1,0:T(4,128)(2,1)S(1)}, bf16[4,1024]{1,0:T(4,128)(2,1)}, u32[]{:S(2)}) copy-start(bf16[4,1024]{1,0:T(4,128)(2,1)} %param.21) | copy-start | bytes 24580
  32.8 10.0 %copy-start.12 = (bf16[512]{0:T(512)(128)(2,1)S(1)}, bf16[512]{0:T(512)(128)(2,1)}, u32[]{:S(2)}) copy-start(bf16[512]{0:T(512)(128)(2,1)} %param.26) | copy-start | bytes 3076
  32.8 10.0 %copy-start.10 = (bf16[2048]{0:T(1024)(128)(2,1)S(1)}, bf16[2048]{0:T(1024)(128)(2,1)}, u32[]{:S(2)}) copy-start(bf16[2048]{0:T(1024)(128)(2,1)} %param.28) | copy-start | bytes 12292
  34.7 58.1 %copy-start.4 = (f32[16,1,64,256]{3,0,1,2:T(8,128)}, f32[16,1,64,256]{3,0,1,2:T(8,128)S(1)}, u32[]{:S(2)}) copy-start(f32[16,1,64,256]{3,0,1,2:T(8,128)S(1)} %fusion.42) | copy-start | bytes 3145732
  51.7 8.5 %copy-start.2 = (f32[16,64,1,1024]{3,1,0,2:T(8,128)}, f32[16,64,1,1024]{3,1,0,2:T(8,128)S(1)}, u32[]{:S(2)}) copy-start(f32[16,64,1,1024]{3,1,0,2:T(8,128)S(1)} %fusion.12) | copy-start | bytes 12582916
  92.8 3.7 %copy-start.6 = (bf16[4,257,512]{2,1,0:T(8,128)(2,1)S(1)}, bf16[4,257,512]{2,1,0:T(8,128)(2,1)}, u32[]{:S(2)}) copy-start(bf16[4,257,512]{2,1,0:T(8,128)(2,1)} %shard_map.176) | copy-start | bytes 3158020
  92.9 4.8 %copy-start.3 = (f32[16,64,1,1024]{3,1,0,2:T(8,128)S(1)}, f32[16,64,1,1024]{3,1,0,2:T(8,128)}, u32[]{:S(2)}) copy-start(f32[16,64,1,1024]{3,1,0,2:T(8,128)} %copy-done.2) | copy-start | bytes 12582916
  170.1 10.4 %copy-start.1 = (bf16[512,2048]{1,0:T(8,128)(2,1)S(1)}, bf16[512,2048]{1,0:T(8,128)(2,1)}, u32[]{:S(2)}) copy-start(bf16[512,2048]{1,0:T(8,128)(2,1)} %param.27) | copy-start | bytes 6291460
Sparse Core Ops, SparseCore 0:
  10.2 88.3 all-gather.2
  100.6 58.4 all-gather.4

commit v4 on v3

--- a/solution.py
+++ b/solution.py
@@ -148,12 +148,14 @@
     )(value)
 
 
-def recurrence_kernel(decay_ref, carried_ref, terms_ref, raised_ref, out_ref, inter_ref, state_ref):
+def recurrence_kernel(
+    decay_ref, carried_ref, weighted_ref, value_ref, raised_ref, out_ref, inter_ref, state_ref
+):
     step = pl.program_id(0)
-    chunk = terms_ref.shape[0]
-    reach = terms_ref.shape[-1] // decay_ref.shape[-1]
+    chunk = weighted_ref.shape[0]
     heads = raised_ref.shape[1]
     keys = raised_ref.shape[-1]
+    reach = value_ref.shape[-1] // decay_ref.shape[-1]
 
     @pl.when(step == 0)
     def _():
@@ -161,40 +163,56 @@
 
     for page in range(chunk):
         kept = jnp.concatenate([carried_ref[page]] * reach, axis=-1) * state_ref[...]
+        fading = jnp.concatenate([decay_ref[page]] * reach, axis=-1)
         for head in range(heads):
+            rows = slice(head * keys, (head + 1) * keys)
             inter_ref[page, head] = jnp.dot(
                 raised_ref[page, head],
-                kept[head * keys : (head + 1) * keys],
+                kept[rows],
                 preferred_element_type=jnp.float32,
                 precision=lax.Precision.HIGHEST,
             )
-        state = jnp.concatenate([decay_ref[page]] * reach, axis=-1) * kept + terms_ref[page]
-        state_ref[...] = state
-        out_ref[page] = state
-
-
-def page_recurrence(decay, carried, terms, raised, chunk=4):
-    page_count, rows, width = terms.shape
+            term = jnp.dot(
+                weighted_ref[page, head],
+                value_ref[page, head],
+                preferred_element_type=jnp.float32,
+                precision=lax.Precision.HIGHEST,
+            )
+            state = fading[rows] * kept[rows] + term
+            state_ref[rows, :] = state
+            out_ref[page, rows, :] = state
+
+
+def page_recurrence(decay, carried, weighted, values, raised, chunk=4):
+    page_count, heads, keys, length = weighted.shape
+    width = values.shape[-1]
+    rows = heads * keys
     lanes = decay.shape[-1]
-    heads, length = raised.shape[1], raised.shape[2]
-    block = pl.BlockSpec((chunk, rows, width), lambda p: (p, 0, 0))
     flags = pl.BlockSpec((chunk, rows, lanes), lambda p: (p, 0, 0))
+
+    def pages(shape):
+        return pl.BlockSpec((chunk,) + shape, lambda p: (p, 0, 0, 0))
+
     return pl.pallas_call(
         recurrence_kernel,
         out_shape=(
-            jax.ShapeDtypeStruct(terms.shape, terms.dtype),
+            jax.ShapeDtypeStruct((page_count, rows, width), jnp.float32),
             jax.ShapeDtypeStruct((page_count, heads, length, width), jnp.float32),
         ),
         grid=(page_count // chunk,),
         in_specs=[
             flags,
             flags,
-            block,
-            pl.BlockSpec((chunk,) + raised.shape[1:], lambda p: (p, 0, 0, 0)),
+            pages((heads, keys, length)),
+            pages((heads, length, width)),
+            pages((heads, length, keys)),
         ],
-        out_specs=(block, pl.BlockSpec((chunk, heads, length, width), lambda p: (p, 0, 0, 0))),
+        out_specs=(
+            pl.BlockSpec((chunk, rows, width), lambda p: (p, 0, 0)),
+            pages((heads, length, width)),
+        ),
         scratch_shapes=[pltpu.VMEM((rows, width), jnp.float32)],
-    )(decay, carried, terms, raised)
+    )(decay, carried, weighted, values, raised)
 
 
 def rms_scaled(values, scale_gain):
@@ -255,18 +273,16 @@
     layer_output = jnp.einsum("phij,phjv->phiv", scores, value_matrix, precision=TOP_PRECISION)
     closing_sum = decay_sum[:, :, -1, :]
     weighted_rows = key_rows * jnp.exp(closing_sum[:, :, None, :] - decay_sum)
-    page_terms = jnp.einsum(
-        "phte,phtb->pheb", weighted_rows, value_matrix, precision=TOP_PRECISION
-    )
     lanes = 128
     rows = closing_sum.shape[1] * closing_sum.shape[2]
     memories, inter_output = page_recurrence(
         jnp.broadcast_to(jnp.exp(closing_sum).reshape(page_count, rows, 1), (page_count, rows, lanes)),
         jnp.broadcast_to(carried[:, None, None], (page_count, rows, lanes)),
-        page_terms.reshape(page_count, rows, page_terms.shape[-1]),
+        weighted_rows.transpose(0, 1, 3, 2),
+        value_matrix,
         raised_rows,
     )
-    memories = memories.reshape(page_terms.shape)
+    memories = memories.reshape(closing_sum.shape + (value_matrix.shape[-1],))
     layer_output = layer_output + inter_output
     return memories[-1], layer_output, memories
 

time: 189 us -> 195 us (1.032)
  matrix products: 69.8 us -> 63.6 us
  Pallas kernels: 39.8 us -> 45.1 us
  local copies, waits for them, and re-layouts: 12.2 us -> 17 us
  other arithmetic: 45.9 us -> 48.4 us
    dot_general x1 -> x0, matrix products: 6.17 us -> none  [page_block(): jnp.einsum('phte,phtb->pheb', weighted_rows, value_matrix, precision=TOP_...]
    pallas_call x1, Pallas kernels: 11.2 us -> 17.1 us  [page_recurrence(): pl.pallas_call(recurrence_kernel, out_shape=(jax.ShapeDtypeStruct((page_c...]
    transpose x0 -> x2, local copies, waits for them, and re-layouts: none -> 4.69 us  [the longest x1 3.19 us: page_block(): weighted_rows.transpose(0, 1, 3, 2)]
  transfers between devices with their start and end apart: 3 -> 3, of which waited for: 1 -> 0; matrix products, arithmetic and copies ran while one was open for 58% -> 56% of each run, Pallas kernels for 19% -> 21%
where the time goes in v4:
time: 195 us; the launch traced here: 193 us
  matrix products  63.6 us (33%)
  other arithmetic  48.4 us (25%)
  Pallas kernels  45.1 us (23%)
  local copies, waits for them, and re-layouts  17 us (9%)
  between operations  14.5 us (7%)
  starting transfers between devices  4.45 us (2%)
    dot_general x1, matrix products, widen(): return jnp.dot(feed_in, weight_rows, preferred_element_type=jnp.float32)  17.7 us
    pallas_call x1, Pallas kernels, page_recurrence(): pl.pallas_call(recurrence_kernel, out_shape=(jax.ShapeDtypeStruct((page_c...  17.1 us
    pallas_call x1, Pallas kernels, spread_over_seq(): pl.pallas_call(spread_kernel, out_shape=jax.ShapeDtypeStruct((count,) + v...  15.3 us
    pallas_call x2, Pallas kernels, from_partner(): pl.pallas_call(functools.partial(partner_kernel, rows), out_shape=jax.Sha...  12.7 us
    reduce_sum x2, other arithmetic, rms_scaled(): jnp.mean(values * values, axis=-1, keepdims=True) + EPSILON  11.3 us
    dot_general x1, matrix products, on_device(): lax.dot_general(hidden, down_rows, (((1,), (1,)), ((), ())), preferred_el...  10.9 us
    reshape x1, other arithmetic, on_device(): short_conv(by_page, before, carried, conv_weight)  8.02 us
    dot_general x1, matrix products, on_device(): jnp.dot(normed, project_weight, preferred_element_type=jnp.float32)  7.26 us
  transfers between devices with their start and end apart: 3, of which 0 were waited for; matrix products, arithmetic and copies ran while one was open for 56% of the time, Pallas kernels for 21%

profile of v4, /device:TPU:1, one launch (start us, length us, event | category | flops | bytes accessed | tf_op | source)
XLA Modules:
  0.0 193.3 jit_solution(10172161172691109260)
XLA Ops:
  7.2 2.1 %pad_maximum_fusion.1 = bf16[128,2816]{1,0:T(8,128)(2,1)} fusion(bf16[128,1408]{1,0:T(8,128)(2,1)} %param.30, bf16[128,1408]{1,0:T(8,128)(2,1)} %param.29), kind=kLoop, calls=%fused_computation.79 | loop fusion | flops 1441792 | bytes 1441792 | tf_op jit(solution)/shard_map/concatenate | solution.py:387
  10.3 3.3 %fusion.3 = f32[1024]{0:T(1024)S(1)} fusion(bf16[1024,2048]{1,0:T(8,128)(2,1)} %param.18), kind=kLoop, calls=%fused_computation.10 | loop fusion | flops 6290432 | bytes 4198400 | tf_op jit(solution)/shard_map/reduce_sum | solution.py:222
  13.6 7.3 %convolution_convert_fusion.2 = bf16[1024,1024]{1,0:T(8,128)(2,1)S(1)} fusion(bf16[2048,1024]{1,0:T(8,128)(2,1)} %param.20, bf16[1024,2048]{1,0:T(8,128)(2,1)S(1)} %copy-done.5, f32[2048]{0:T(1024)S(1)} %convert_element_type.151, f32[1024]{0:T(1024)S(1)} %add_rsqrt_fusion.2), kind=kOutput, calls=%fused_computation.50 | convolution fusion | flops 4304404480 | bytes 10498048 | tf_op jit(solution)/shard_map/dot_general | solution.py:317
  22.2 4.4 %collective-permute-start = (bf16[3,1024]{1,0:T(4,128)(2,1)S(1)}, bf16[3,1024]{1,0:T(4,128)(2,1)S(1)}, u32[]{:S(2)}, u32[]{:S(2)}) collective-permute-start(bf16[3,1024]{1,0:T(4,128)(2,1)S(1)} %slice_bitcast_fusion.4), channel_id=1, source_target_pairs={{0,2},{2,4},{4,6},{1,3},{3,5},{5,7},{8,10},{10,12},{12,14},{9,11},... | collective-permute-start | bytes 18440 | tf_op jit(solution)/shard_map/ppermute | solution.py:25
  27.6 5.2 %fusion.30 = f32[1024,256]{1,0:T(8,128)} fusion(bf16[16,256]{1,0:T(8,128)(2,1)S(1)} %copy-done.15, bf16[2048,16]{0,1:T(8,128)(2,1)S(1)} %copy-done.14, f32[256]{0:T(256)S(1)} %copy-done.16, bf16[1024,2048]{1,0:T(8,128)(2,1)} %param.18, f32[2048]{0:T(1024)S(1)} %convert_element_type.151, f32[1024]{0:T(1024)S(1)} %add_rsqrt_fusion.2), kind=kOutput, calls=%fused_computation.56 | convolution fusion | flops 86523904 | bytes 5329920 | tf_op jit(solution)/shard_map/dot_general | solution.py:330
  37.8 4.1 %convert_element_type.154 = f32[16,64,1024]{2,1,0:T(8,128)} convert(bf16[16,64,1024]{2,1,0:T(8,128)(2,1)} %bitcast.140) | non-fusion elementwise | flops 1048576 | bytes 6291456 | tf_op jit(solution)/shard_map/convert_element_type | solution.py:240
  43.7 8.0 %fusion.12 = f32[16,64,1,1024]{3,1,0,2:T(8,128)S(1)} fusion(f32[16,64,1024]{2,1,0:T(8,128)} %convert_element_type.154, f32[16,3,1024]{2,1,0:T(4,128)S(1)} %convert_multiply_fusion.4, f32[1024]{0:T(1024)S(1)} %bitcast.147, f32[1024]{0:T(1024)S(1)} %bitcast.148, f32[1024]{0:T(1024)S(1)} %bitcast.146, f32[1024]{0:T(1024)S(1)} %bitcast.145), kind=kLoop, calls=%fused_computation.25 | loop fusion | flops 10485760 | bytes 8601600 | tf_op jit(solution)/shard_map/reshape | solution.py:323
  51.7 2.4 %bitcast_multiply_fusion.1.raised_ref = f32[16,1,64,256]{3,2,1,0:T(8,128)} fusion(f32[16,1,64,256]{3,0,1,2:T(8,128)S(1)} %fusion.39, f32[16,64,1,1024]{3,1,0,2:T(8,128)S(1)} %fusion.12), kind=kLoop, calls=%fused_computation.57 | loop fusion | flops 1310720 | bytes 3145728 | tf_op jit(solution)/shard_map/mul | solution.py:267
  57.5 3.2 %copy.52.weighted_ref = f32[16,1,256,64]{3,2,1,0:T(8,128)} copy(f32[16,1,256,64]{2,3,0,1:T(8,128)} %fusion.36) | data formatting | bytes 2097152 | tf_op jit(solution)/shard_map/transpose | solution.py:281
  64.2 17.1 %shard_map.175 = (f32[16,256,512]{2,1,0:T(8,128)}, f32[16,1,64,512]{3,2,1,0:T(8,128)}) custom-call(f32[16,256,128]{2,1,0:T(8,128)} %broadcast_in_dim.38.decay_ref, f32[16,256,128]{2,1,0:T(8,128)} %broadcast_in_dim.39.carried_ref, f32[16,1,256,64]{3,2,1,0:T(8,128)} %copy.52.weighted_ref, f32[16,1,64,512]{3,2,1,0:T(8,128)} %slice_bitcast_fusion.value_ref, ...), custom_call_target="tpu_custom_call" | custom-call | tf_op jit(solution)/shard_map/pallas_call | solution.py:196
  83.0 15.3 %shard_map.176 = bf16[4,257,512]{2,1,0:T(8,128)(2,1)} custom-call(bf16[257,512]{1,0:T(8,128)(2,1)} %fusion.49.src_ref), custom_call_target="tpu_custom_call" | custom-call | tf_op jit(solution)/shard_map/pallas_call | solution.py:138
  99.1 3.7 %convolution_select_fusion = f32[16,64,64]{2,1,0:T(8,128)S(1)} fusion(f32[16,1,64,256]{3,0,1,2:T(8,128)S(1)} %fusion.39, pred[64,64]{1,0:T(8,128)(4,1)S(1)} %iota_compare_fusion.1, f32[16,64,1,1024]{3,1,0,2:T(8,128)} %copy-done.2), kind=kOutput, calls=%fused_computation.53 | convolution fusion | flops 103874560 | bytes 4464640 | tf_op jit(solution)/shard_map/phik,phjk->phij/dot_general | solution.py:269
  103.9 2.4 %fusion.25 = f32[16,64,512]{2,1,0:T(8,128)} fusion(f32[16,64,64]{2,1,0:T(8,128)S(1)} %convolution_select_fusion, f32[16,64,1,1024]{3,1,0,2:T(8,128)S(1)} %copy-done.3), kind=kOutput, calls=%fused_computation.45 | convolution fusion | flops 201326592 | bytes 4718592 | tf_op jit(solution)/shard_map/phij,phjv->phiv/dot_general | solution.py:273
  106.5 5.9 %multiply_reduce_fusion = (f32[16,64]{1,0:T(8,128)S(1)}, f32[16,1,64,512]{3,2,1,0:T(8,128)}) fusion(f32[16,1,64,256]{3,0,1,2:T(8,128)} %copy-done.4, f32[16,256]{1,0:T(8,128)S(1)} %get-tuple-element.88, f32[16]{0:T(128)S(1)} %reduce.2, f32[16,64,1,1024]{3,1,0,2:T(8,128)} %copy-done.2, f32[1,256,512]{2,1,0:T(8,128)S(1)} %get-tuple-element.51, ...), kind=kOutput, calls=%fused_computation.47 | convolution fusion | flops 809237504 | bytes 8933440 | tf_op jit(solution)/shard_map/dlof,lfg->dlog/dot_general | solution.py:356
  112.6 6.2 %fusion.24 = bf16[1024,512]{1,0:T(8,128)(2,1)S(1)} fusion(f32[16,1,64,512]{3,2,1,0:T(8,128)} %get-tuple-element.95, f32[512]{0:T(512)S(1)} %convert_element_type.164, f32[1024]{0:T(1024)S(1)} %rsqrt.29, bf16[2048,512]{1,0:T(8,128)(2,1)} %param.25, bf16[1024,2048]{1,0:T(8,128)(2,1)} %param.18, f32[2048]{0:T(1024)S(1)} %convert_element_type.151, ...), kind=kOutput, calls=%fused_computation.43 | convolution fusion | flops 2160066560 | bytes 9455616 | tf_op jit(solution)/shard_map/dot_general | solution.py:364
  118.7 4.4 %convolution_convert_fusion.1.src_ref = bf16[1024,2048]{1,0:T(8,128)(2,1)} fusion(bf16[1024,512]{1,0:T(8,128)(2,1)S(1)} %fusion.24, bf16[512,2048]{1,0:T(8,128)(2,1)S(1)} %copy-done), kind=kOutput, calls=%fused_computation.37 | convolution fusion | flops 2149580800 | bytes 7340032 | tf_op jit(solution)/shard_map/dot_general | solution.py:370
  123.1 8.2 %shard_map.177 = bf16[1024,2048]{1,0:T(8,128)(2,1)} custom-call(bf16[1024,2048]{1,0:T(8,128)(2,1)} %convolution_convert_fusion.1.src_ref), custom_call_target="tpu_custom_call" | custom-call | tf_op jit(solution)/shard_map/pallas_call | solution.py:77
  131.3 8.0 %fusion = (f32[1024]{0:T(1024)S(1)}, bf16[1024,2048]{1,0:T(8,128)(2,1)}) fusion(bf16[1024,2048]{1,0:T(8,128)(2,1)} %shard_map.177, bf16[1024,2048]{1,0:T(8,128)(2,1)} %convolution_convert_fusion.1.src_ref, bf16[1024,2048]{1,0:T(8,128)(2,1)} %param.18), kind=kLoop, calls=%fused_computation.7 | loop fusion | flops 18873344 | bytes 16781312 | tf_op jit(solution)/shard_map/reduce_sum | solution.py:222
  139.4 5.4 %fusion.16 = bf16[16,1,256,512]{3,2,1,0:T(8,128)(2,1)} fusion(f32[16,256,512]{2,1,0:T(8,128)} %get-tuple-element.50, f32[256,512]{1,0:T(8,128)S(1)} %bitcast.137, f32[16,256]{1,0:T(8,128)S(1)} %bitcast_multiply_fusion.7), kind=kLoop, calls=%fused_computation.29 | loop fusion | flops 6291456 | bytes 13123584
  144.8 17.7 %fusion.17 = f32[1024,2816]{1,0:T(8,128)S(1)} fusion(bf16[2048,2816]{1,0:T(8,128)(2,1)} %all-gather.3.cloned.1.call-done, bf16[1024,2048]{1,0:T(8,128)(2,1)} %get-tuple-element.87, f32[2048]{0:T(1024)S(1)} %convert_element_type.172, f32[1024]{0:T(1024)S(1)} %add_rsqrt_fusion.1), kind=kOutput, calls=%fused_computation.30 | convolution fusion | flops 11819548672 | bytes 27275264 | tf_op jit(solution)/shard_map/dot_general | solution.py:382
  162.5 2.9 %fusion.7 = bf16[1024,1408]{1,0:T(8,128)(2,1)} fusion(f32[1024,2816]{1,0:T(8,128)S(1)} %fusion.17), kind=kLoop, calls=%fused_computation.18 | loop fusion | flops 8650752 | bytes 14417920 | tf_op jit(solution)/shard_map/convert_element_type | solution.py:392
  165.4 10.9 %convolution_convert_fusion.src_ref = bf16[1024,2048]{1,0:T(8,128)(2,1)} fusion(bf16[1024,1408]{1,0:T(8,128)(2,1)} %fusion.7, bf16[2048,1408]{1,0:T(8,128)(2,1)} %all-gather.5.cloned.1.call-done), kind=kOutput, calls=%fused_computation.36 | convolution fusion | flops 5907677184 | bytes 12845056 | tf_op jit(solution)/shard_map/dot_general | solution.py:395
  176.3 4.5 %shard_map.178 = bf16[512,2048]{1,0:T(8,128)(2,1)} custom-call(bf16[1024,2048]{1,0:T(8,128)(2,1)} %convolution_convert_fusion.src_ref), custom_call_target="tpu_custom_call" | custom-call | tf_op jit(solution)/shard_map/pallas_call | solution.py:77
  180.9 5.6 %add_convert_fusion.1 = bf16[512,2048]{1,0:T(8,128)(2,1)} fusion(bf16[512,2048]{1,0:T(8,128)(2,1)} %shard_map.178, bf16[1024,2048]{1,0:T(8,128)(2,1)} %convolution_convert_fusion.src_ref, s32[]{:T(128)S(6)} %select_n.32, bf16[1024,2048]{1,0:T(8,128)(2,1)} %get-tuple-element.87), kind=kLoop, calls=%fused_computation.33 | loop fusion | flops 6291456 | bytes 8388612 | tf_op jit(solution)/shard_map/convert_element_type | solution.py:402
  (83 shorter events, 20.7 us)
Async XLA Ops:
  7.2 111.6 %copy-start = (bf16[512,2048]{1,0:T(8,128)(2,1)S(1)}, bf16[512,2048]{1,0:T(8,128)(2,1)}, u32[]{:S(2)}) copy-start(bf16[512,2048]{1,0:T(8,128)(2,1)} %param.27) | copy-start | bytes 6291460
  7.2 137.6 %all-gather.3.cloned.1.call-start = ((), (), s32[]{:S(2)}) async-start(), calls=%async_computation | async-start | bytes 12255232 | tf_op jit(solution)/shard_map/all_gather | solution.py:386
  9.4 156.0 %all-gather.5.cloned.1.call-start = ((), (), s32[]{:S(2)}) async-start(), calls=%async_computation.1 | async-start | bytes 6127616 | tf_op jit(solution)/shard_map/all_gather | solution.py:394
  9.4 4.1 %copy-start.5 = (bf16[1024,2048]{1,0:T(8,128)(2,1)S(1)}, bf16[1024,2048]{1,0:T(8,128)(2,1)}, u32[]{:S(2)}) copy-start(bf16[1024,2048]{1,0:T(8,128)(2,1)} %param.18) | copy-start | bytes 12582916
  13.6 13.0 %copy-start.8 = (bf16[1408,128]{1,0:T(8,128)(2,1)S(1)}, bf16[1408,128]{1,0:T(8,128)(2,1)}, u32[]{:S(2)}) copy-start(bf16[1408,128]{1,0:T(8,128)(2,1)} %param.31) | copy-start | bytes 1081348
  13.6 14.0 %copy-start.14 = (bf16[2048,16]{0,1:T(8,128)(2,1)S(1)}, bf16[2048,16]{0,1:T(8,128)(2,1)}, u32[]{:S(2)}) copy-start(bf16[2048,16]{0,1:T(8,128)(2,1)} %param.22) | copy-start | bytes 196612
  13.6 14.0 %copy-start.15 = (bf16[16,256]{1,0:T(8,128)(2,1)S(1)}, bf16[16,256]{1,0:T(8,128)(2,1)}, u32[]{:S(2)}) copy-start(bf16[16,256]{1,0:T(8,128)(2,1)} %param.23) | copy-start | bytes 24580
  13.6 14.0 %copy-start.16 = (f32[256]{0:T(256)S(1)}, f32[256]{0:T(256)}, u32[]{:S(2)}) copy-start(f32[256]{0:T(256)} %param.24) | copy-start | bytes 3076
  20.9 1.3 copy-start.7
  22.2 21.4 %collective-permute-start = (bf16[3,1024]{1,0:T(4,128)(2,1)S(1)}, bf16[3,1024]{1,0:T(4,128)(2,1)S(1)}, u32[]{:S(2)}, u32[]{:S(2)}) collective-permute-start(bf16[3,1024]{1,0:T(4,128)(2,1)S(1)} %slice_bitcast_fusion.4), channel_id=1, source_target_pairs={{0,2},{2,4},{4,6},{1,3},{3,5},{5,7},{8,10},{10,12},{12,14},{9,11},... | collective-permute-start | bytes 18440 | tf_op jit(solution)/shard_map/ppermute | solution.py:25
  27.6 7.2 %copy-start.11 = (s32[1,16]{1,0:T(1,128)S(1)}, s32[1,16]{1,0:T(1,128)}, u32[]{:S(2)}) copy-start(s32[1,16]{1,0:T(1,128)} %param.33) | copy-start | bytes 196
  27.6 7.2 %copy-start.13 = (s32[1,16]{1,0:T(1,128)S(1)}, s32[1,16]{1,0:T(1,128)}, u32[]{:S(2)}) copy-start(s32[1,16]{1,0:T(1,128)} %param.32) | copy-start | bytes 196
  27.6 7.3 %copy-start.9 = (bf16[4,1024]{1,0:T(4,128)(2,1)S(1)}, bf16[4,1024]{1,0:T(4,128)(2,1)}, u32[]{:S(2)}) copy-start(bf16[4,1024]{1,0:T(4,128)(2,1)} %param.21) | copy-start | bytes 24580
  32.8 10.0 %copy-start.12 = (bf16[512]{0:T(512)(128)(2,1)S(1)}, bf16[512]{0:T(512)(128)(2,1)}, u32[]{:S(2)}) copy-start(bf16[512]{0:T(512)(128)(2,1)} %param.26) | copy-start | bytes 3076
  32.8 10.0 %copy-start.10 = (bf16[2048]{0:T(1024)(128)(2,1)S(1)}, bf16[2048]{0:T(1024)(128)(2,1)}, u32[]{:S(2)}) copy-start(bf16[2048]{0:T(1024)(128)(2,1)} %param.28) | copy-start | bytes 12292
  34.7 64.3 %copy-start.4 = (f32[16,1,64,256]{3,0,1,2:T(8,128)}, f32[16,1,64,256]{3,0,1,2:T(8,128)S(1)}, u32[]{:S(2)}) copy-start(f32[16,1,64,256]{3,0,1,2:T(8,128)S(1)} %fusion.39) | copy-start | bytes 3145732
  51.7 3.9 %copy-start.2 = (f32[16,64,1,1024]{3,1,0,2:T(8,128)}, f32[16,64,1,1024]{3,1,0,2:T(8,128)S(1)}, u32[]{:S(2)}) copy-start(f32[16,64,1,1024]{3,1,0,2:T(8,128)S(1)} %fusion.12) | copy-start | bytes 12582916
  99.1 3.7 %copy-start.6 = (bf16[4,257,512]{2,1,0:T(8,128)(2,1)S(1)}, bf16[4,257,512]{2,1,0:T(8,128)(2,1)}, u32[]{:S(2)}) copy-start(bf16[4,257,512]{2,1,0:T(8,128)(2,1)} %shard_map.176) | copy-start | bytes 3158020
  99.1 4.8 %copy-start.3 = (f32[16,64,1,1024]{3,1,0,2:T(8,128)S(1)}, f32[16,64,1,1024]{3,1,0,2:T(8,128)}, u32[]{:S(2)}) copy-start(f32[16,64,1,1024]{3,1,0,2:T(8,128)} %copy-done.2) | copy-start | bytes 12582916
  176.3 10.1 %copy-start.1 = (bf16[512,2048]{1,0:T(8,128)(2,1)S(1)}, bf16[512,2048]{1,0:T(8,128)(2,1)}, u32[]{:S(2)}) copy-start(bf16[512,2048]{1,0:T(8,128)(2,1)} %param.27) | copy-start | bytes 6291460
Sparse Core Ops, SparseCore 0:
  10.2 88.3 all-gather.2
  100.6 58.4 all-gather.4

commit v5 on v3

--- a/solution.py
+++ b/solution.py
@@ -16,7 +16,7 @@
 
 
 EPSILON = 1e-06
-TOP_PRECISION = lax.Precision.HIGH
+TOP_PRECISION = lax.Precision.DEFAULT
 
 
 def shifted(value, axis, steps):

time: 189 us -> 188 us (level)
  matrix products: 69.8 us -> 67.1 us
    dot_general x1 -> x0, matrix products: 3.71 us -> none  [page_block(): jnp.einsum('phik,phjk->phij', raised_rows, lowered, precision=TOP_PRECISION)]
    dot_general x1, matrix products: 2.36 us -> 5.44 us  [page_block(): jnp.einsum('phij,phjv->phiv', scores, value_matrix, precision=TOP_PRECISION)]
  transfers between devices with their start and end apart: 3 -> 3, of which waited for: 1 -> 1; matrix products, arithmetic and copies ran while one was open for 58% -> 57% of each run, Pallas kernels for 19% -> 19%
where the time goes in v5:
time: 188 us; the launch traced here: 187 us
  matrix products  67.1 us (36%)
  other arithmetic  46.3 us (25%)
  Pallas kernels  39.5 us (21%)
  between operations  14.4 us (8%)
  local copies, waits for them, and re-layouts  13.5 us (7%)
  starting transfers between devices  4.63 us (2%)
    dot_general x1, matrix products, widen(): return jnp.dot(feed_in, weight_rows, preferred_element_type=jnp.float32)  17.7 us
    pallas_call x1, Pallas kernels, spread_over_seq(): pl.pallas_call(spread_kernel, out_shape=jax.ShapeDtypeStruct((count,) + v...  15.4 us
    pallas_call x2, Pallas kernels, from_partner(): pl.pallas_call(functools.partial(partner_kernel, rows), out_shape=jax.Sha...  13 us
    pallas_call x1, Pallas kernels, page_recurrence(): pl.pallas_call(recurrence_kernel, out_shape=(jax.ShapeDtypeStruct(terms.s...  11 us
    dot_general x1, matrix products, on_device(): lax.dot_general(hidden, down_rows, (((1,), (1,)), ((), ())), preferred_el...  10.9 us
    reduce_sum x2, other arithmetic, rms_scaled(): jnp.mean(values * values, axis=-1, keepdims=True) + EPSILON  10.5 us
    reshape x1, other arithmetic, on_device(): short_conv(by_page, before, carried, conv_weight)  7.85 us
    dot_general x1, matrix products, on_device(): jnp.dot(normed, project_weight, preferred_element_type=jnp.float32)  7.26 us
  transfers between devices with their start and end apart: 3, of which 1 were waited for; matrix products, arithmetic and copies ran while one was open for 57% of the time, Pallas kernels for 19%

profile of v5, /device:TPU:1, one launch (start us, length us, event | category | flops | bytes accessed | tf_op | source)
XLA Modules:
  0.0 187.3 jit_solution(7321053182328478536)
XLA Ops:
  7.2 2.1 %pad_maximum_fusion.1 = bf16[128,2816]{1,0:T(8,128)(2,1)} fusion(bf16[128,1408]{1,0:T(8,128)(2,1)} %param.30, bf16[128,1408]{1,0:T(8,128)(2,1)} %param.29), kind=kLoop, calls=%fused_computation.80 | loop fusion | flops 1441792 | bytes 1441792 | tf_op jit(solution)/shard_map/concatenate | solution.py:371
  10.3 3.3 %fusion.3 = f32[1024]{0:T(1024)S(1)} fusion(bf16[1024,2048]{1,0:T(8,128)(2,1)} %param.18), kind=kLoop, calls=%fused_computation.10 | loop fusion | flops 6290432 | bytes 4198400 | tf_op jit(solution)/shard_map/reduce_sum | solution.py:204
  13.6 7.3 %convolution_convert_fusion.2 = bf16[1024,1024]{1,0:T(8,128)(2,1)S(1)} fusion(bf16[2048,1024]{1,0:T(8,128)(2,1)} %param.20, bf16[1024,2048]{1,0:T(8,128)(2,1)S(1)} %copy-done.4, f32[2048]{0:T(1024)S(1)} %convert_element_type.151, f32[1024]{0:T(1024)S(1)} %add_rsqrt_fusion.2), kind=kOutput, calls=%fused_computation.49 | convolution fusion | flops 4304404480 | bytes 10498048 | tf_op jit(solution)/shard_map/dot_general | solution.py:301
  22.2 4.6 %collective-permute-start = (bf16[3,1024]{1,0:T(4,128)(2,1)S(1)}, bf16[3,1024]{1,0:T(4,128)(2,1)S(1)}, u32[]{:S(2)}, u32[]{:S(2)}) collective-permute-start(bf16[3,1024]{1,0:T(4,128)(2,1)S(1)} %slice_bitcast_fusion.6), channel_id=1, source_target_pairs={{0,2},{2,4},{4,6},{1,3},{3,5},{5,7},{8,10},{10,12},{12,14},{9,11},... | collective-permute-start | bytes 18440 | tf_op jit(solution)/shard_map/ppermute | solution.py:25
  27.8 5.2 %fusion.29 = f32[1024,256]{1,0:T(8,128)} fusion(bf16[16,256]{1,0:T(8,128)(2,1)S(1)} %copy-done.13, bf16[2048,16]{0,1:T(8,128)(2,1)S(1)} %copy-done.12, f32[256]{0:T(256)S(1)} %copy-done.14, bf16[1024,2048]{1,0:T(8,128)(2,1)} %param.18, f32[2048]{0:T(1024)S(1)} %convert_element_type.151, f32[1024]{0:T(1024)S(1)} %add_rsqrt_fusion.2), kind=kOutput, calls=%fused_computation.55 | convolution fusion | flops 86523904 | bytes 5329920 | tf_op jit(solution)/shard_map/dot_general | solution.py:314
  37.9 4.1 %convert_element_type.154 = f32[16,64,1024]{2,1,0:T(8,128)} convert(bf16[16,64,1024]{2,1,0:T(8,128)(2,1)} %bitcast.150) | non-fusion elementwise | flops 1048576 | bytes 6291456 | tf_op jit(solution)/shard_map/convert_element_type | solution.py:222
  43.9 7.9 %fusion.12 = f32[16,64,1,1024]{3,1,0,2:T(8,128)S(1)} fusion(f32[16,64,1024]{2,1,0:T(8,128)} %convert_element_type.154, f32[16,3,1024]{2,1,0:T(4,128)S(1)} %convert_multiply_fusion.4, f32[1024]{0:T(1024)S(1)} %bitcast.157, f32[1024]{0:T(1024)S(1)} %bitcast.158, f32[1024]{0:T(1024)S(1)} %bitcast.156, f32[1024]{0:T(1024)S(1)} %bitcast.155), kind=kLoop, calls=%fused_computation.25 | loop fusion | flops 10485760 | bytes 8601600 | tf_op jit(solution)/shard_map/reshape | solution.py:307
  51.8 2.4 %bitcast_multiply_fusion.1.raised_ref = f32[16,1,64,256]{3,2,1,0:T(8,128)} fusion(f32[16,1,64,256]{3,0,1,2:T(8,128)S(1)} %fusion.45, f32[16,64,1,1024]{3,1,0,2:T(8,128)S(1)} %fusion.12), kind=kLoop, calls=%fused_computation.61 | loop fusion | flops 1310720 | bytes 3145728 | tf_op jit(solution)/shard_map/mul | solution.py:249
  54.1 4.9 %fusion.25.terms_ref = f32[16,256,512]{2,1,0:T(8,128)} fusion(f32[16,64,1,1024]{3,1,0,2:T(8,128)S(1)} %fusion.12, f32[16,1,64,256]{3,0,1,2:T(8,128)S(1)} %fusion.45, f32[16,256]{1,0:T(8,128)S(1)} %get-tuple-element.89), kind=kOutput, calls=%fused_computation.47 | convolution fusion | flops 270270464 | bytes 12599296 | tf_op jit(solution)/shard_map/phte,phtb->pheb/dot_general | solution.py:258
  62.5 11.0 %shard_map.175 = (f32[16,256,512]{2,1,0:T(8,128)}, f32[16,1,64,512]{3,2,1,0:T(8,128)}) custom-call(f32[16,256,128]{2,1,0:T(8,128)} %broadcast_in_dim.38.decay_ref, f32[16,256,128]{2,1,0:T(8,128)} %broadcast_in_dim.39.carried_ref, f32[16,256,512]{2,1,0:T(8,128)} %fusion.25.terms_ref, f32[16,1,64,256]{3,2,1,0:T(8,128)} %bitcast_multiply_fusion.1.raised_ref), custom_call_target="tpu_custom_call" | custom-call | tf_op jit(solution)/shard_map/pallas_call | solution.py:182
  75.3 15.4 %shard_map.176 = bf16[4,257,512]{2,1,0:T(8,128)(2,1)} custom-call(bf16[257,512]{1,0:T(8,128)(2,1)} %fusion.56.src_ref), custom_call_target="tpu_custom_call" | custom-call | tf_op jit(solution)/shard_map/pallas_call | solution.py:138
  90.7 2.3 %slice_bitcast_fusion.3 = bf16[4,1,256,512]{3,2,1,0:T(8,128)(2,1)} fusion(bf16[4,257,512]{2,1,0:T(8,128)(2,1)} %shard_map.176), kind=kLoop, calls=%fused_computation.74 | loop fusion | bytes 2097152 | tf_op jit(solution)/shard_map/while | solution.py:53
  93.7 5.4 %fusion.26 = f32[16,64,512]{2,1,0:T(8,128)} fusion(f32[16,64,1,1024]{3,1,0,2:T(8,128)} %copy-done.2, f32[16,1,64,256]{3,0,1,2:T(8,128)S(1)} %fusion.45, pred[64,64]{1,0:T(8,128)(4,1)S(1)} %iota_compare_fusion.1), kind=kOutput, calls=%fused_computation.48 | convolution fusion | flops 103874560 | bytes 8396800 | tf_op jit(solution)/shard_map/phij,phjv->phiv/dot_general | solution.py:255
  99.4 5.2 %multiply_reduce_fusion = (f32[16,64]{1,0:T(8,128)S(1)}, f32[16,1,64,512]{3,2,1,0:T(8,128)}) fusion(f32[16,1,64,256]{3,0,1,2:T(8,128)} %copy-done.3, f32[16,256]{1,0:T(8,128)S(1)} %get-tuple-element.88, f32[16]{0:T(128)S(1)} %reduce.2, f32[16,64,1,1024]{3,1,0,2:T(8,128)} %copy-done.2, f32[16,1,64,512]{3,2,1,0:T(8,128)} %get-tuple-element.49, ...), kind=kOutput, calls=%fused_computation.46 | convolution fusion | flops 272366592 | bytes 8933440 | tf_op jit(solution)/shard_map/dlof,lfg->dlog/dot_general | solution.py:340
  104.7 6.1 %fusion.24 = bf16[1024,512]{1,0:T(8,128)(2,1)S(1)} fusion(f32[16,1,64,512]{3,2,1,0:T(8,128)} %get-tuple-element.95, f32[512]{0:T(512)S(1)} %convert_element_type.164, f32[1024]{0:T(1024)S(1)} %rsqrt.29, bf16[2048,512]{1,0:T(8,128)(2,1)} %param.25, bf16[1024,2048]{1,0:T(8,128)(2,1)} %param.18, f32[2048]{0:T(1024)S(1)} %convert_element_type.151, ...), kind=kOutput, calls=%fused_computation.44 | convolution fusion | flops 2160066560 | bytes 9455616 | tf_op jit(solution)/shard_map/dot_general | solution.py:348
  110.9 4.4 %convolution_convert_fusion.1.src_ref = bf16[1024,2048]{1,0:T(8,128)(2,1)} fusion(bf16[1024,512]{1,0:T(8,128)(2,1)S(1)} %fusion.24, bf16[512,2048]{1,0:T(8,128)(2,1)S(1)} %copy-done), kind=kOutput, calls=%fused_computation.37 | convolution fusion | flops 2149580800 | bytes 7340032 | tf_op jit(solution)/shard_map/dot_general | solution.py:354
  115.2 8.2 %shard_map.177 = bf16[1024,2048]{1,0:T(8,128)(2,1)} custom-call(bf16[1024,2048]{1,0:T(8,128)(2,1)} %convolution_convert_fusion.1.src_ref), custom_call_target="tpu_custom_call" | custom-call | tf_op jit(solution)/shard_map/pallas_call | solution.py:77
  123.5 7.3 %fusion = (f32[1024]{0:T(1024)S(1)}, bf16[1024,2048]{1,0:T(8,128)(2,1)}) fusion(bf16[1024,2048]{1,0:T(8,128)(2,1)} %shard_map.177, bf16[1024,2048]{1,0:T(8,128)(2,1)} %convolution_convert_fusion.1.src_ref, bf16[1024,2048]{1,0:T(8,128)(2,1)} %param.18), kind=kLoop, calls=%fused_computation.7 | loop fusion | flops 18873344 | bytes 16781312 | tf_op jit(solution)/shard_map/reduce_sum | solution.py:204
  130.7 6.0 %fusion.16 = bf16[16,1,256,512]{3,2,1,0:T(8,128)(2,1)} fusion(f32[16,256,512]{2,1,0:T(8,128)} %get-tuple-element.50, f32[256,512]{1,0:T(8,128)S(1)} %bitcast.147, f32[16,256]{1,0:T(8,128)S(1)} %bitcast_multiply_fusion.7), kind=kLoop, calls=%fused_computation.29 | loop fusion | flops 6291456 | bytes 13123584
  136.8 17.7 %fusion.17 = f32[1024,2816]{1,0:T(8,128)S(1)} fusion(bf16[2048,2816]{1,0:T(8,128)(2,1)} %all-gather.3.cloned.1.call-done, bf16[1024,2048]{1,0:T(8,128)(2,1)} %get-tuple-element.87, f32[2048]{0:T(1024)S(1)} %convert_element_type.172, f32[1024]{0:T(1024)S(1)} %add_rsqrt_fusion.1), kind=kOutput, calls=%fused_computation.30 | convolution fusion | flops 11819548672 | bytes 27275264 | tf_op jit(solution)/shard_map/dot_general | solution.py:366
  154.5 3.0 %fusion.7 = bf16[1024,1408]{1,0:T(8,128)(2,1)} fusion(f32[1024,2816]{1,0:T(8,128)S(1)} %fusion.17), kind=kLoop, calls=%fused_computation.18 | loop fusion | flops 8650752 | bytes 14417920 | tf_op jit(solution)/shard_map/convert_element_type | solution.py:376
  159.1 10.9 %convolution_convert_fusion.src_ref = bf16[1024,2048]{1,0:T(8,128)(2,1)} fusion(bf16[1024,1408]{1,0:T(8,128)(2,1)} %fusion.7, bf16[2048,1408]{1,0:T(8,128)(2,1)} %all-gather.5.cloned.1.call-done), kind=kOutput, calls=%fused_computation.36 | convolution fusion | flops 5907677184 | bytes 12845056 | tf_op jit(solution)/shard_map/dot_general | solution.py:379
  170.1 4.8 %shard_map.178 = bf16[512,2048]{1,0:T(8,128)(2,1)} custom-call(bf16[1024,2048]{1,0:T(8,128)(2,1)} %convolution_convert_fusion.src_ref), custom_call_target="tpu_custom_call" | custom-call | tf_op jit(solution)/shard_map/pallas_call | solution.py:77
  174.9 5.6 %add_convert_fusion.1 = bf16[512,2048]{1,0:T(8,128)(2,1)} fusion(bf16[512,2048]{1,0:T(8,128)(2,1)} %shard_map.178, bf16[1024,2048]{1,0:T(8,128)(2,1)} %convolution_convert_fusion.src_ref, s32[]{:T(128)S(6)} %select_n.32, bf16[1024,2048]{1,0:T(8,128)(2,1)} %get-tuple-element.87), kind=kLoop, calls=%fused_computation.33 | loop fusion | flops 6291456 | bytes 8388612 | tf_op jit(solution)/shard_map/convert_element_type | solution.py:386
  (76 shorter events, 18.0 us)
Async XLA Ops:
  7.2 103.7 %copy-start = (bf16[512,2048]{1,0:T(8,128)(2,1)S(1)}, bf16[512,2048]{1,0:T(8,128)(2,1)}, u32[]{:S(2)}) copy-start(bf16[512,2048]{1,0:T(8,128)(2,1)} %param.27) | copy-start | bytes 6291460
  7.2 129.6 %all-gather.3.cloned.1.call-start = ((), (), s32[]{:S(2)}) async-start(), calls=%async_computation | async-start | bytes 12255232 | tf_op jit(solution)/shard_map/all_gather | solution.py:370
  9.4 149.7 %all-gather.5.cloned.1.call-start = ((), (), s32[]{:S(2)}) async-start(), calls=%async_computation.1 | async-start | bytes 6127616 | tf_op jit(solution)/shard_map/all_gather | solution.py:378
  9.4 4.1 %copy-start.4 = (bf16[1024,2048]{1,0:T(8,128)(2,1)S(1)}, bf16[1024,2048]{1,0:T(8,128)(2,1)}, u32[]{:S(2)}) copy-start(bf16[1024,2048]{1,0:T(8,128)(2,1)} %param.18) | copy-start | bytes 12582916
  13.6 13.2 %copy-start.6 = (bf16[1408,128]{1,0:T(8,128)(2,1)S(1)}, bf16[1408,128]{1,0:T(8,128)(2,1)}, u32[]{:S(2)}) copy-start(bf16[1408,128]{1,0:T(8,128)(2,1)} %param.31) | copy-start | bytes 1081348
  13.6 14.2 %copy-start.12 = (bf16[2048,16]{0,1:T(8,128)(2,1)S(1)}, bf16[2048,16]{0,1:T(8,128)(2,1)}, u32[]{:S(2)}) copy-start(bf16[2048,16]{0,1:T(8,128)(2,1)} %param.22) | copy-start | bytes 196612
  13.6 14.2 %copy-start.13 = (bf16[16,256]{1,0:T(8,128)(2,1)S(1)}, bf16[16,256]{1,0:T(8,128)(2,1)}, u32[]{:S(2)}) copy-start(bf16[16,256]{1,0:T(8,128)(2,1)} %param.23) | copy-start | bytes 24580
  13.6 14.2 %copy-start.14 = (f32[256]{0:T(256)S(1)}, f32[256]{0:T(256)}, u32[]{:S(2)}) copy-start(f32[256]{0:T(256)} %param.24) | copy-start | bytes 3076
  20.9 1.3 copy-start.5
  22.2 21.6 %collective-permute-start = (bf16[3,1024]{1,0:T(4,128)(2,1)S(1)}, bf16[3,1024]{1,0:T(4,128)(2,1)S(1)}, u32[]{:S(2)}, u32[]{:S(2)}) collective-permute-start(bf16[3,1024]{1,0:T(4,128)(2,1)S(1)} %slice_bitcast_fusion.6), channel_id=1, source_target_pairs={{0,2},{2,4},{4,6},{1,3},{3,5},{5,7},{8,10},{10,12},{12,14},{9,11},... | collective-permute-start | bytes 18440 | tf_op jit(solution)/shard_map/ppermute | solution.py:25
  27.8 7.2 %copy-start.9 = (s32[1,16]{1,0:T(1,128)S(1)}, s32[1,16]{1,0:T(1,128)}, u32[]{:S(2)}) copy-start(s32[1,16]{1,0:T(1,128)} %param.33) | copy-start | bytes 196
  27.8 7.2 %copy-start.11 = (s32[1,16]{1,0:T(1,128)S(1)}, s32[1,16]{1,0:T(1,128)}, u32[]{:S(2)}) copy-start(s32[1,16]{1,0:T(1,128)} %param.32) | copy-start | bytes 196
  27.8 7.3 %copy-start.7 = (bf16[4,1024]{1,0:T(4,128)(2,1)S(1)}, bf16[4,1024]{1,0:T(4,128)(2,1)}, u32[]{:S(2)}) copy-start(bf16[4,1024]{1,0:T(4,128)(2,1)} %param.21) | copy-start | bytes 24580
  33.0 10.0 %copy-start.10 = (bf16[512]{0:T(512)(128)(2,1)S(1)}, bf16[512]{0:T(512)(128)(2,1)}, u32[]{:S(2)}) copy-start(bf16[512]{0:T(512)(128)(2,1)} %param.26) | copy-start | bytes 3076
  33.0 10.0 %copy-start.8 = (bf16[2048]{0:T(1024)(128)(2,1)S(1)}, bf16[2048]{0:T(1024)(128)(2,1)}, u32[]{:S(2)}) copy-start(bf16[2048]{0:T(1024)(128)(2,1)} %param.28) | copy-start | bytes 12292
  34.9 58.8 %copy-start.3 = (f32[16,1,64,256]{3,0,1,2:T(8,128)}, f32[16,1,64,256]{3,0,1,2:T(8,128)S(1)}, u32[]{:S(2)}) copy-start(f32[16,1,64,256]{3,0,1,2:T(8,128)S(1)} %fusion.45) | copy-start | bytes 3145732
  51.8 7.3 %copy-start.2 = (f32[16,64,1,1024]{3,1,0,2:T(8,128)}, f32[16,64,1,1024]{3,1,0,2:T(8,128)S(1)}, u32[]{:S(2)}) copy-start(f32[16,64,1,1024]{3,1,0,2:T(8,128)S(1)} %fusion.12) | copy-start | bytes 12582916
  170.0 10.4 %copy-start.1 = (bf16[512,2048]{1,0:T(8,128)(2,1)S(1)}, bf16[512,2048]{1,0:T(8,128)(2,1)}, u32[]{:S(2)}) copy-start(bf16[512,2048]{1,0:T(8,128)(2,1)} %param.27) | copy-start | bytes 6291460
Sparse Core Ops, SparseCore 0:
  10.2 88.3 all-gather.2
  100.6 58.4 all-gather.4
